TPU v7x, 32 devices: a whole 2x2x4 slice. The times are simulated.
32 devices in a mesh: groups: 2 (over x), pen: 16 (over z, y, core).
Axes of the slice: x: 2, y: 2, z: 4, core: 2. Of those that a mesh axis runs over, the one named last changes fastest.
Arguments:
- point_feat: bfloat16 [64, 65536], P(None, ('groups', 'pen')), parts along dimension 1, may hold values from -6 to 6
- pair_kernel: bfloat16 [2048, 128, 128], P(('groups', 'pen')), parts along dimension 0, may hold values from -0.5 to 0.5
- pair_owner: int32 [2048, 1], P(('groups', 'pen')), parts along dimension 0, may hold values from 0 to 15; in each aligned block of 64 rows (0 to 63, 64 to 127, ...) at most 8 rows name the same one
- pair_block: int32 [2048], P(('groups', 'pen')), parts along dimension 0, may hold values from 0 to 255
- spec_weight: bfloat16 [2, 256, 16, 64, 128], P(None, 'pen'), may hold values from -3 to 3
- mlp_up: bfloat16 [2, 256, 64], replicated, may hold values from -0.75 to 0.75
- mlp_down: bfloat16 [2, 64, 256], replicated, may hold values from -0.375 to 0.375
Outputs:
- point_out: float32 [64, 65536], P(None, ('groups', 'pen')), parts along dimension 1
There are 2 independent parts, one for each index of `groups`. A program takes and returns all parts, laid end to end along the dimension named above; an argument that names none is the same for every part. Nothing has to cross between parts.
Inputs may be any that keep to these rules, and one draw needn't show every extreme that they name: `pair_owner`: among the pairs of one device, no device is named more than 8 times.
All inputs are finite; a program needn't handle non-finite values.
Results may differ from a plain program's by a relative error of at most 0.0055.
Values may be sent and summed in bfloat16 or wider, within the bound.
A program may use at most 128 MiB of HBM per device.

v0:
```python
import math

import jax
import jax.numpy as jnp
from jax import lax
from jax.sharding import PartitionSpec as P

NX = 128
NY = 64
NZ = 64
MX = 16
MY = 16
MZ = 16
LAYERS = 2
NBR = 4


HIGHEST = lax.Precision.HIGHEST


def yz_tables():
    mode_index = jnp.arange(MY * MZ, dtype=jnp.int32)
    wave_y = mode_index // MZ - MY // 2
    wave_z = mode_index % MZ
    cell_index = jnp.arange(NY * NZ, dtype=jnp.int32)
    row_y = cell_index // NZ
    row_z = cell_index % NZ
    phase_turns = (
        jnp.mod(row_y[:, None] * wave_y[None, :], NY).astype(jnp.float32) / NY
        + jnp.mod(row_z[:, None] * wave_z[None, :], NZ).astype(jnp.float32) / NZ
    )
    angle = 2.0 * math.pi * phase_turns
    forward_table = jnp.stack([jnp.cos(angle), -jnp.sin(angle)], axis=2).reshape(
        NY * NZ, 2 * MY * MZ
    )
    scaling = jnp.where(wave_z == 0, 1.0, 2.0).astype(jnp.float32) / (NX * NY * NZ)
    inverse_table = forward_table * jnp.repeat(scaling, 2)[None, :]
    return (forward_table, inverse_table)


def along_tables(positions):
    wave_number = jnp.arange(MX, dtype=jnp.int32) - MX // 2
    angle = (
        2.0
        * math.pi
        * jnp.mod(wave_number[:, None] * positions[None, :], NX).astype(jnp.float32)
        / NX
    )
    return (jnp.cos(angle), jnp.sin(angle))


def mix_modes(modes_real, modes_imag, weight_real, weight_imag):
    mixed_real = jnp.einsum(
        "mjc,mjco->mjo", modes_real, weight_real, precision=HIGHEST
    ) - jnp.einsum("mjc,mjco->mjo", modes_imag, weight_imag, precision=HIGHEST)
    mixed_imag = jnp.einsum(
        "mjc,mjco->mjo", modes_real, weight_imag, precision=HIGHEST
    ) + jnp.einsum("mjc,mjco->mjo", modes_imag, weight_real, precision=HIGHEST)
    return (mixed_real, mixed_imag)


def unfold_modes(mixed_real, mixed_imag, cosine_table, sine_table):
    back_real = jnp.einsum("jx,mjo->oxm", cosine_table, mixed_real, precision=HIGHEST) - jnp.einsum(
        "jx,mjo->oxm", sine_table, mixed_imag, precision=HIGHEST
    )
    back_imag = jnp.einsum("jx,mjo->oxm", sine_table, mixed_real, precision=HIGHEST) + jnp.einsum(
        "jx,mjo->oxm", cosine_table, mixed_imag, precision=HIGHEST
    )
    stacked = jnp.stack([back_real, back_imag], axis=3)
    return stacked.reshape(stacked.shape[0], stacked.shape[1], 2 * stacked.shape[2])


def spectral_part(grid_field, weights_now, forward_table, inverse_table, planes):
    channels = grid_field.shape[0]
    modes_all = forward_table.shape[1] // 2
    modes_here = weights_now.shape[0]
    planar = jnp.dot(
        grid_field.reshape(channels * planes, NY * NZ), forward_table, precision=HIGHEST
    ).reshape(channels, planes, 2 * modes_all)
    weight_real = weights_now[..., :channels].astype(jnp.float32)
    weight_imag = weights_now[..., channels:].astype(jnp.float32)
    across = lax.all_to_all(planar, "pen", split_axis=2, concat_axis=1, tiled=True).reshape(
        channels, NX, modes_here, 2
    )
    cosine_table, sine_table = along_tables(jnp.arange(NX, dtype=jnp.int32))
    part_real = across[..., 0]
    part_imag = across[..., 1]
    modes_real = jnp.einsum("jx,cxm->mjc", cosine_table, part_real, precision=HIGHEST) + jnp.einsum(
        "jx,cxm->mjc", sine_table, part_imag, precision=HIGHEST
    )
    modes_imag = jnp.einsum("jx,cxm->mjc", cosine_table, part_imag, precision=HIGHEST) - jnp.einsum(
        "jx,cxm->mjc", sine_table, part_real, precision=HIGHEST
    )
    mixed_real, mixed_imag = mix_modes(modes_real, modes_imag, weight_real, weight_imag)
    joined = unfold_modes(mixed_real, mixed_imag, cosine_table, sine_table)
    result = lax.all_to_all(joined, "pen", split_axis=1, concat_axis=2, tiled=True)
    flat_result = result.reshape(channels * planes, 2 * modes_all)
    return jnp.dot(flat_result, inverse_table.T, precision=HIGHEST).reshape(
        channels, planes * NY * NZ
    )


def channel_mlp(summed, weight_up, weight_down):
    rounded = summed.astype(jnp.bfloat16)
    hidden = jnp.dot(weight_up, rounded, preferred_element_type=jnp.float32)
    active = jax.nn.gelu(hidden, approximate=True).astype(jnp.bfloat16)
    return summed + jnp.dot(weight_down, active, preferred_element_type=jnp.float32)


def per_device(point_feat, pair_kernel, pair_owner, pair_block, spec_weight, mlp_up, mlp_down):
    devices = lax.axis_size("pen")
    pair_count = pair_kernel.shape[0]
    block_size = pair_kernel.shape[1]
    channels = point_feat.shape[0]
    capacity = 2 * pair_count // devices
    slots_total = devices * capacity
    planes = NX // devices
    local_cells = planes * NY * NZ
    grid_count = local_cells // block_size
    owners = pair_owner[:, 0]
    member = (owners[:, None] == jnp.arange(devices, dtype=jnp.int32)[None, :]).astype(jnp.int32)
    earlier = jnp.sum((jnp.cumsum(member, axis=0) - member) * member, axis=1)
    slot_index = owners * capacity + earlier
    slot_target = (
        jnp.zeros((slots_total,), jnp.int32)
        .at[slot_index]
        .set(pair_block)
        .reshape(devices, capacity)
    )
    feature_blocks = point_feat.reshape(channels, pair_count // NBR, block_size).transpose(1, 0, 2)
    pair_features = jnp.repeat(feature_blocks, NBR, axis=0)
    contrib_pairs = jnp.einsum(
        "pci,pij->pcj", pair_features, pair_kernel, preferred_element_type=jnp.float32
    )
    send_sums = (
        jnp.zeros((slots_total, channels, block_size), jnp.float32)
        .at[slot_index]
        .set(contrib_pairs)
    )
    got_sums, got_targets = (
        lax.all_to_all(
            send_sums.reshape(devices, capacity, channels, block_size),
            "pen",
            split_axis=0,
            concat_axis=0,
            tiled=True,
        ),
        lax.all_to_all(slot_target, "pen", split_axis=0, concat_axis=0, tiled=True),
    )
    flat_targets = got_targets.reshape(slots_total)
    contrib = got_sums.reshape(slots_total, channels, block_size)
    grid_blocks = jax.ops.segment_sum(contrib, flat_targets, num_segments=grid_count)
    grid_field = grid_blocks.transpose(1, 0, 2).reshape(channels, local_cells)
    forward_table, inverse_table = yz_tables()
    for number in range(LAYERS):
        spectral = spectral_part(
            grid_field, spec_weight[number], forward_table, inverse_table, planes
        )
        summed = grid_field + spectral
        grid_field = channel_mlp(summed, mlp_up[number], mlp_down[number])
    grid_out = (
        grid_field.astype(jnp.bfloat16).reshape(channels, grid_count, block_size).transpose(1, 0, 2)
    )
    fetched = lax.all_to_all(
        grid_out[lax.all_to_all(slot_target, "pen", split_axis=0, concat_axis=0, tiled=True)],
        "pen",
        split_axis=0,
        concat_axis=0,
        tiled=True,
    )
    pair_rows = fetched.reshape(slots_total, channels, block_size)[slot_index]
    pair_results = jnp.einsum(
        "pcj,pij->pci", pair_rows, pair_kernel, preferred_element_type=jnp.float32
    )
    summed_back = pair_results.reshape(pair_count // NBR, NBR, channels, block_size).sum(axis=1)
    return summed_back.transpose(1, 0, 2).reshape(channels, pair_count // NBR * block_size)


def solution(mesh):
    in_specs = (
        P(None, ("groups", "pen")),
        P(("groups", "pen"), None, None),
        P(("groups", "pen"), None),
        P(("groups", "pen")),
        P(None, "pen", None, None, None),
        P(),
        P(),
    )
    out_specs = P(None, ("groups", "pen"))
    return jax.shard_map(
        per_device, mesh=mesh, in_specs=in_specs, out_specs=out_specs, check_vma=False
    )
```

profile of v0, /device:TPU:1, one launch (start us, length us, event | category | flops | bytes accessed | tf_op | source)
XLA Modules:
  0.0 649.1 jit_solution(12362412406866547493)
XLA Ops:
  4.1 7.3 %all-to-all-start = ((s32[16,1,8]{2,1,0:T(1,128)}), s32[16,1,8]{2,1,0:T(1,128)S(1)}, u32[]{:S(2)}, u32[]{:S(2)}) async-start(s32[16,1,8]{2,1,0:T(1,128)} %bitcast.3), calls=%async_computation | async-start | bytes 16384 | tf_op jit(solution)/shard_map/all_to_all | solution.py:148
  17.3 10.1 %scatter_fusion = f32[128,64,128]{2,1,0:T(8,128)} fusion(f32[128,64,128]{2,1,0:T(8,128)} %broadcast_in_dim.18, s32[64]{0:T(128)S(1)} %fusion.155, f32[64,64,128]{2,1,0:T(8,128)} %fusion.232), kind=kCustom, calls=%fused_computation.3 | custom fusion | bytes 6291712 | tf_op jit(solution)/shard_map/scatter | solution.py:138
  27.4 6.3 all-to-all-start.1
  33.8 18.7 %fusion.58 = (f32[4096,256,1]{1,0,2:T(8,128)S(1)}, f32[4096,256,1]{1,0,2:T(8,128)S(1)}) fusion(s32[256]{0:T(256)S(1)} %get-tuple-element.17, s32[4096]{0:T(1024)S(1)} %get-tuple-element.15, s32[256]{0:T(256)S(1)} %get-tuple-element.18, s32[4096]{0:T(1024)S(1)} %get-tuple-element.16), kind=kLoop, calls=%fused_computation.82 | loop fusion | flops 30408704 | bytes 8423424 | tf_op jit(solution)/shard_map/cos | solution.py:33
  52.5 6.5 broadcast_multiply_fusion
  58.9 13.4 %copy.142 = f32[4096,256,2]{0,2,1:T(2,128)} copy(f32[4096,256,2]{1,0,2:T(8,128)} %get-tuple-element.8) | data formatting | bytes 16777216 | tf_op jit(solution)/shard_map/stack | solution.py:33
  72.3 11.1 %reshape.465 = f32[4096,512]{0,1:T(8,128)} reshape(f32[4096,256,2]{0,2,1:T(2,128)} %copy.142) | data formatting | bytes 16777216 | tf_op jit(solution)/shard_map/reshape | solution.py:33
  84.7 27.0 %all-to-all-done.1 = f32[16,8,64,128]{3,2,1,0:T(8,128)} async-done(((f32[16,8,64,128]{3,2,1,0:T(8,128)}), f32[16,8,64,128]{3,2,1,0:T(8,128)}, u32[]{:S(2)}, u32[]{:S(2)}) %all-to-all-start.1) | async-done | bytes 4194336 | tf_op jit(solution)/shard_map/all_to_all | solution.py:141
  111.7 4.3 broadcast_in_dim.16
  116.0 22.5 %scatter_fusion.1 = f32[256,64,128]{2,1,0:T(8,128)} fusion(f32[256,64,128]{2,1,0:T(8,128)} %broadcast_in_dim.16, s32[128]{0:T(128)S(1)} %reshape.513, f32[128,64,128]{2,1,0:T(8,128)} %bitcast.7), kind=kCustom, calls=%fused_computation.4 | custom fusion | flops 1048576 | bytes 12583424 | tf_op jit(solution)/shard_map/scatter-add | solution.py:152
  138.5 11.5 %copy.140 = f32[64,256,128]{2,1,0:T(8,128)} copy(f32[64,256,128]{2,0,1:T(8,128)} %bitcast.268) | data formatting | bytes 16777216 | tf_op jit(solution)/shard_map/transpose | solution.py:153
  149.9 9.3 %dot_general.115 = f32[64,8,4096]{2,1,0:T(8,128)} reshape(f32[64,256,128]{2,1,0:T(8,128)} %copy.140) | data formatting | bytes 16777216 | tf_op jit(solution)/shard_map/dot_general | solution.py:77
  159.2 16.4 %fusion.21 = f32[64,8,512]{2,1,0:T(8,128)S(1)} fusion(f32[64,8,4096]{2,1,0:T(8,128)} %dot_general.115, f32[4096,512]{0,1:T(8,128)} %reshape.465), kind=kOutput, calls=%fused_computation.34 | convolution fusion | flops 12884901888 | bytes 17825792 | tf_op jit(solution)/shard_map/dot_general | solution.py:77
  178.0 3.8 reshape.548
  181.8 19.2 %all-to-all-start.2 = ((f32[16,1,16384]{2,1,0:T(1,128)}), f32[16,1,16384]{2,1,0:T(1,128)S(1)}, u32[]{:S(2)}, u32[]{:S(2)}) async-start(f32[16,1,16384]{2,1,0:T(1,128)} %reshape.548), calls=%async_computation.2 | async-start | bytes 2097152 | tf_op jit(solution)/shard_map/all_to_all | solution.py:82
  201.0 6.9 %slice_bitcast_fusion = (bf16[16,16,64,128]{3,2,1,0:T(8,128)(2,1)}, bf16[16,16,64,128]{3,2,1,0:T(8,128)(2,1)}) fusion(bf16[2,16,16,64,128]{4,3,2,1,0:T(8,128)(2,1)} %param.11), kind=kLoop, calls=%fused_computation.60 | loop fusion | bytes 16777216 | tf_op jit(solution)/shard_map/squeeze | solution.py:157
  208.0 16.2 %all-to-all-done.2 = f32[16,1,16384]{2,1,0:T(1,128)S(1)} async-done(((f32[16,1,16384]{2,1,0:T(1,128)}), f32[16,1,16384]{2,1,0:T(1,128)S(1)}, u32[]{:S(2)}, u32[]{:S(2)}) %all-to-all-start.2) | async-done | bytes 1048608 | tf_op jit(solution)/shard_map/all_to_all | solution.py:82
  225.7 4.3 reduce.4
  243.6 5.5 fusion.51
  249.1 3.6 fusion.49
  253.7 5.8 fusion.47
  273.5 7.1 %all-to-all-start.3 = ((f32[16,1,16384]{2,1,0:T(1,128)}), f32[16,1,16384]{2,1,0:T(1,128)}, u32[]{:S(2)}, u32[]{:S(2)}) async-start(f32[16,1,16384]{2,1,0:T(1,128)} %reshape.550), calls=%async_computation.3 | async-start | bytes 2097152 | tf_op jit(solution)/shard_map/all_to_all | solution.py:96
  280.6 13.4 %copy.152 = f32[4096,256,2]{0,2,1:T(2,128)} copy(f32[4096,256,2]{1,0,2:T(8,128)} %get-tuple-element.7) | data formatting | bytes 16777216 | tf_op jit(solution)/shard_map/mul | solution.py:37
  294.0 10.9 %mul.262 = f32[4096,512]{0,1:T(8,128)} reshape(f32[4096,256,2]{0,2,1:T(2,128)} %copy.152) | data formatting | bytes 16777216 | tf_op jit(solution)/shard_map/mul | solution.py:37
  304.9 4.3 reduce.5
  311.4 5.7 copy.151
  320.6 17.3 %fusion.233 = f32[512,4096]{1,0:T(8,128)} fusion(f32[512,512]{1,0:T(8,128)S(1)} %reshape.468, f32[4096,512]{0,1:T(8,128)} %mul.262), kind=kOutput, calls=%fused_computation.269 | convolution fusion | flops 12884901888 | bytes 17825792 | tf_op jit(solution)/shard_map/dot_general | solution.py:98
  337.9 9.3 %reshape.470 = f32[64,256,128]{2,1,0:T(8,128)} reshape(f32[512,4096]{1,0:T(8,128)} %fusion.233) | data formatting | bytes 16777216 | tf_op jit(solution)/shard_map/reshape | solution.py:98
  347.2 9.4 %reshape.469 = f32[64,32768]{1,0:T(8,128)} reshape(f32[512,4096]{1,0:T(8,128)} %fusion.233) | data formatting | bytes 16777216 | tf_op jit(solution)/shard_map/reshape | solution.py:98
  356.6 30.0 %fusion = f32[64,32768]{1,0:T(8,128)} fusion(f32[64,32768]{1,0:T(8,128)} %reshape.469, bf16[2,64,256]{2,1,0:T(8,128)(2,1)S(1)} %copy-done.10, bf16[2,256,64]{1,2,0:T(8,128)(2,1)S(1)} %copy-done.11, f32[256,64,128]{2,1,0:T(8,128)} %scatter_fusion.1, f32[64,256,128]{2,1,0:T(8,128)} %reshape.470), kind=kOutput, calls=%fused_computation.11 | convolution fusion | flops 2231369728 | bytes 42008576 | tf_op jit(solution)/shard_map/dot_general | solution.py:107
  386.5 8.1 %copy.195 = f32[8,8,8,4096]{3,2,1,0:T(8,128)S(1)} copy(f32[8,8,8,4096]{3,1,2,0:T(8,128)} %bitcast.278) | data formatting | bytes 16777216
  394.7 16.0 %fusion.19 = f32[64,8,512]{2,1,0:T(8,128)S(1)} fusion(f32[64,8,4096]{2,1,0:T(8,128)S(1)} %bitcast.269, f32[4096,512]{0,1:T(8,128)} %reshape.465), kind=kOutput, calls=%fused_computation.32 | convolution fusion | flops 12884901888 | bytes 17825792 | tf_op jit(solution)/shard_map/dot_general | solution.py:77
  415.7 31.4 %all_to_all.83 = f32[16,1,16384]{2,1,0:T(1,128)} all-to-all(f32[16,1,16384]{2,1,0:T(1,128)S(1)} %reshape.552), channel_id=1, replica_groups=mesh['groups'=2,'pen'=16] {'pen'}, dimensions={0} | all-to-all | bytes 2097152 | tf_op jit(solution)/shard_map/all_to_all | solution.py:82
  447.1 4.3 reduce.6
  465.1 5.8 fusion.43
  470.9 3.6 fusion.41
  475.4 5.8 fusion.39
  495.2 4.8 all-to-all-start.5
  500.3 22.9 %all-to-all-done.5 = f32[16,1,16384]{2,1,0:T(1,128)} async-done(((f32[16,1,16384]{2,1,0:T(1,128)}), f32[16,1,16384]{2,1,0:T(1,128)}, u32[]{:S(2)}, u32[]{:S(2)}) %all-to-all-start.5) | async-done | bytes 1048608 | tf_op jit(solution)/shard_map/all_to_all | solution.py:96
  523.2 4.3 reduce.7
  529.7 5.7 copy.163
  538.9 17.3 %fusion.234 = f32[512,4096]{1,0:T(8,128)} fusion(f32[512,512]{1,0:T(8,128)S(1)} %reshape.473, f32[4096,512]{0,1:T(8,128)} %mul.262), kind=kOutput, calls=%fused_computation.270 | convolution fusion | flops 12884901888 | bytes 17825792 | tf_op jit(solution)/shard_map/dot_general | solution.py:98
  556.2 9.4 %reshape.474 = f32[64,32768]{1,0:T(8,128)} reshape(f32[512,4096]{1,0:T(8,128)} %fusion.234) | data formatting | bytes 16777216 | tf_op jit(solution)/shard_map/reshape | solution.py:98
  565.6 20.8 %fusion.55 = bf16[8,256,8,128]{3,2,1,0:T(8,128)(2,1)} fusion(f32[64,32768]{1,0:T(8,128)} %fusion, f32[64,32768]{1,0:T(8,128)} %reshape.474, bf16[2,64,256]{2,1,0:T(8,128)(2,1)S(1)} %copy-done.10, bf16[2,256,64]{1,2,0:T(8,128)(2,1)S(1)} %copy-done.11), kind=kOutput, calls=%fused_computation.80 | convolution fusion | flops 2233466880 | bytes 37814272 | tf_op jit(solution)/shard_map/dot_general | solution.py:107
  586.4 5.3 copy.212
  591.7 4.3 gather_fusion
  596.0 6.5 %all-to-all-start.6 = ((bf16[16,8,64,128]{3,2,1,0:T(8,128)(2,1)}), bf16[16,8,64,128]{3,2,1,0:T(8,128)(2,1)}, u32[]{:S(2)}, u32[]{:S(2)}) async-start(bf16[16,8,64,128]{3,2,1,0:T(8,128)(2,1)} %bitcast.279), calls=%async_computation.6 | async-start | bytes 4194304 | tf_op jit(solution)/shard_map/all_to_all | solution.py:164
  602.5 41.6 %all-to-all-done.6 = bf16[16,8,64,128]{3,2,1,0:T(8,128)(2,1)} async-done(((bf16[16,8,64,128]{3,2,1,0:T(8,128)(2,1)}), bf16[16,8,64,128]{3,2,1,0:T(8,128)(2,1)}, u32[]{:S(2)}, u32[]{:S(2)}) %all-to-all-start.6) | async-done | bytes 2097184 | tf_op jit(solution)/shard_map/all_to_all | solution.py:164
  (101 shorter events, 93.3 us)
Async XLA Ops:
  0.0 12.7 %copy-start = (bf16[64,128,128]{2,1,0:T(8,128)(2,1)S(1)}, bf16[64,128,128]{2,1,0:T(8,128)(2,1)}, u32[]{:S(2)}) copy-start(bf16[64,128,128]{2,1,0:T(8,128)(2,1)} %param.8) | copy-start | bytes 6291460
  2.5 14.8 %copy-start.8 = (s32[64]{0:T(128)}, s32[64]{0:T(128)S(1)}, u32[]{:S(2)}) copy-start(s32[64]{0:T(128)S(1)} %fusion.155) | copy-start | bytes 772
  4.1 23.3 %all-to-all-start = ((s32[16,1,8]{2,1,0:T(1,128)}), s32[16,1,8]{2,1,0:T(1,128)S(1)}, u32[]{:S(2)}, u32[]{:S(2)}) async-start(s32[16,1,8]{2,1,0:T(1,128)} %bitcast.3), calls=%async_computation | async-start | bytes 16384 | tf_op jit(solution)/shard_map/all_to_all | solution.py:148
  27.4 84.3 %all-to-all-start.1 = ((f32[16,8,64,128]{3,2,1,0:T(8,128)}), f32[16,8,64,128]{3,2,1,0:T(8,128)}, u32[]{:S(2)}, u32[]{:S(2)}) async-start(f32[16,8,64,128]{3,2,1,0:T(8,128)} %bitcast.270), calls=%async_computation.1 | async-start | bytes 8388608 | tf_op jit(solution)/shard_map/all_to_all | solution.py:141
  181.8 42.4 %all-to-all-start.2 = ((f32[16,1,16384]{2,1,0:T(1,128)}), f32[16,1,16384]{2,1,0:T(1,128)S(1)}, u32[]{:S(2)}, u32[]{:S(2)}) async-start(f32[16,1,16384]{2,1,0:T(1,128)} %reshape.548), calls=%async_computation.2 | async-start | bytes 2097152 | tf_op jit(solution)/shard_map/all_to_all | solution.py:82
  224.2 1.0 copy-start.1
  243.6 5.5 copy-start.4
  243.6 9.1 %copy-start.7 = (f32[64,16,16]{2,1,0:T(8,128)S(1)}, f32[64,16,16]{2,1,0:T(8,128)}, u32[]{:S(2)}) copy-start(f32[64,16,16]{2,1,0:T(8,128)} %fusion.77) | copy-start | bytes 196612
  253.7 5.8 copy-start.5
  273.5 31.4 %all-to-all-start.3 = ((f32[16,1,16384]{2,1,0:T(1,128)}), f32[16,1,16384]{2,1,0:T(1,128)}, u32[]{:S(2)}, u32[]{:S(2)}) async-start(f32[16,1,16384]{2,1,0:T(1,128)} %reshape.550), calls=%async_computation.3 | async-start | bytes 2097152 | tf_op jit(solution)/shard_map/all_to_all | solution.py:96
  347.2 9.4 %copy-start.10 = (bf16[2,64,256]{2,1,0:T(8,128)(2,1)S(1)}, bf16[2,64,256]{2,1,0:T(8,128)(2,1)}, u32[]{:S(2)}) copy-start(bf16[2,64,256]{2,1,0:T(8,128)(2,1)} %param.13) | copy-start | bytes 196612
  347.2 9.4 %copy-start.11 = (bf16[2,256,64]{1,2,0:T(8,128)(2,1)S(1)}, bf16[2,256,64]{1,2,0:T(8,128)(2,1)}, u32[]{:S(2)}) copy-start(bf16[2,256,64]{1,2,0:T(8,128)(2,1)} %param.12) | copy-start | bytes 196612
  465.1 5.8 copy-start.2
  465.1 9.4 %copy-start.6 = (f32[64,16,16]{2,1,0:T(8,128)S(1)}, f32[64,16,16]{2,1,0:T(8,128)}, u32[]{:S(2)}) copy-start(f32[64,16,16]{2,1,0:T(8,128)} %fusion.71) | copy-start | bytes 196612
  475.4 5.8 copy-start.3
  495.2 28.0 %all-to-all-start.5 = ((f32[16,1,16384]{2,1,0:T(1,128)}), f32[16,1,16384]{2,1,0:T(1,128)}, u32[]{:S(2)}, u32[]{:S(2)}) async-start(f32[16,1,16384]{2,1,0:T(1,128)} %reshape.554), calls=%async_computation.5 | async-start | bytes 2097152 | tf_op jit(solution)/shard_map/all_to_all | solution.py:96
  591.7 10.8 %copy-start.9 = (s32[64]{0:T(128)S(1)}, s32[64]{0:T(128)}, u32[]{:S(2)}) copy-start(s32[64]{0:T(128)} %copy-done.8) | copy-start | bytes 772
  596.0 48.1 %all-to-all-start.6 = ((bf16[16,8,64,128]{3,2,1,0:T(8,128)(2,1)}), bf16[16,8,64,128]{3,2,1,0:T(8,128)(2,1)}, u32[]{:S(2)}, u32[]{:S(2)}) async-start(bf16[16,8,64,128]{3,2,1,0:T(8,128)(2,1)} %bitcast.279), calls=%async_computation.6 | async-start | bytes 4194304 | tf_op jit(solution)/shard_map/all_to_all | solution.py:164
where the time goes:
time: 660 us; the launch traced here: 649 us
  local copies, waits for them, and re-layouts  215 us (33%)
  matrix products  175 us (27%)
  waiting for transfers between devices  108 us (16%)
  other arithmetic  68.3 us (10%)
  starting transfers between devices  51.2 us (8%)
  blocking collectives  31.4 us (5%)
    dot_general x2, matrix products, channel_mlp(): jnp.dot(weight_down, active, preferred_element_type=jnp.float32)  50.8 us
    all_to_all x1, waiting for transfers between devices, per_device(): lax.all_to_all(grid_out[lax.all_to_all(slot_target, 'pen', split_axis=0,...  41.6 us
    unnamed x38, local copies, waits for them, and re-layouts  38.6 us
    dot_general x2, matrix products, spectral_part(): jnp.dot(flat_result, inverse_table.T, precision=HIGHEST)  34.6 us
    dot_general x2, matrix products, spectral_part(): jnp.dot(grid_field.reshape(channels * planes, NY * NZ), forward_table, pr...  32.4 us
    all_to_all x1, blocking collectives, spectral_part(): lax.all_to_all(planar, 'pen', split_axis=2, concat_axis=1, tiled=True)  31.4 us
    reshape x3, local copies, waits for them, and re-layouts, spectral_part(): jnp.dot(flat_result, inverse_table.T, precision=HIGHEST)  28.1 us
    all_to_all x1, waiting for transfers between devices, per_device(): lax.all_to_all(send_sums.reshape(devices, capacity, channels, block_size)...  27 us
  transfers between devices with their start and end apart: 6, of which 4 were waited for; matrix products, arithmetic and copies ran while one was open for 15% of the time, Pallas kernels for 0%

commit v1 on v0

v1 whole, which is shorter than its diff:
```python
import functools
import math

import jax
import jax.numpy as jnp
import numpy as np
from jax import lax
from jax.experimental import pallas as pl
from jax.experimental.pallas import tpu as pltpu
from jax.sharding import PartitionSpec as P

NX = 128
NY = 64
NZ = 64
MX = 16
MY = 16
MZ = 16
LAYERS = 2
NBR = 4

F32 = jnp.float32
BF16 = jnp.bfloat16
VMEM = pl.BlockSpec(memory_space=pltpu.VMEM)
SMEM = pl.BlockSpec(memory_space=pltpu.SMEM)
NT = (((1,), (1,)), ((), ()))


def plane_table(devices, lanes):
    here = MY * MZ // devices
    row = np.arange(2 * MY * MZ)
    mode = row // (2 * here) * here + row % here
    imag = (row % (2 * here)) // here
    wave_y = mode // MZ - MY // 2
    wave_z = mode % MZ
    cell = np.arange(lanes)
    turns = np.mod(np.outer(wave_y, cell // NZ), NY) / NY + np.mod(np.outer(wave_z, cell % NZ), NZ) / NZ
    first = 2 * np.pi * turns + np.where(imag, np.pi / 2, 0.0)[:, None]
    tiles = NY * NZ // lanes
    step = 2 * np.pi * np.mod(np.outer(np.arange(tiles) * (lanes // NZ), wave_y), NY) / NY
    parts = [np.cos(first), np.sin(first), np.cos(step), np.sin(step)]
    cos0, sin0, cos_k, sin_k = lax.optimization_barrier(tuple(jnp.asarray(a, F32) for a in parts))
    return (cos0[None] * cos_k[:, :, None] - sin0[None] * sin_k[:, :, None]).astype(BF16)


def along_tables(devices):
    planes = NX // devices
    waves = np.arange(MX) - MX // 2
    angle = 2 * np.pi * np.mod(np.outer(waves, np.arange(NX)), NX) / NX
    cos = np.cos(angle).reshape(MX, devices, planes)
    sin = np.sin(angle).reshape(MX, devices, planes)
    to_real = np.stack([cos, sin], axis=2)
    to_imag = np.stack([-sin, cos], axis=2)
    forward = np.concatenate([to_real, to_imag], axis=0).reshape(2 * MX, 2 * NX)
    return jnp.asarray(forward, BF16), jnp.asarray(forward.T, BF16)


def encode_kernel(devices, cap, owner, block, feat, kern, send, slot_of, targets, count):
    pairs = kern.shape[0]
    size = kern.shape[1]

    def clear(d, carry):
        count[d] = 0
        for i in range(cap):
            targets[d * cap + i] = -1
        send[d] = jnp.zeros(send.shape[1:], BF16)
        return carry

    lax.fori_loop(0, devices, clear, 0)

    def one(b, carry):
        values = feat[:, pl.ds(pl.multiple_of(b * size, size), size)]
        for k in range(NBR):
            p = b * NBR + k
            d = owner[p]
            n = count[d]
            count[d] = n + 1
            slot_of[p] = d * cap + n
            targets[d * cap + n] = block[p]
            send[d, n] = jnp.dot(values, kern[p], preferred_element_type=F32).astype(BF16)
        return carry

    lax.fori_loop(0, pairs // NBR, one, 0)
    lane = lax.broadcasted_iota(jnp.int32, (16, size), 1)

    def note(d, carry):
        row = jnp.zeros((16, size), F32)
        for i in range(cap):
            row = jnp.where(lane == i, targets[d * cap + i].astype(F32), row)
        send[d, cap, 0:16, :] = row.astype(BF16)
        return carry

    lax.fori_loop(0, devices, note, 0)


def table_tile(table, k, wide):
    return jnp.concatenate([table[k * wide + i] for i in range(wide)], axis=1)


def gather_sums_kernel(cap, per_plane, wide, targets, got, table, field, spec, total):
    channels, size = got.shape[2], got.shape[3]
    chunk = wide * size
    tiles = table.shape[0] // wide

    def clear(k, carry):
        field[:, pl.ds(pl.multiple_of(k * chunk, chunk), chunk)] = jnp.zeros((field.shape[0], chunk), F32)
        return carry

    lax.fori_loop(0, tiles, clear, 0)

    def add(d, carry):
        for i in range(cap):
            t = targets[d * cap + i]

            @pl.when(t >= 0)
            def _():
                rows = pl.ds(pl.multiple_of(t // per_plane * channels, channels), channels)
                cols = pl.ds(pl.multiple_of(t % per_plane * size, size), size)
                field[rows, cols] += got[d, i].astype(F32)

        return carry

    lax.fori_loop(0, got.shape[0], add, 0)
    total[...] = jnp.zeros_like(total)

    def transform(k, carry):
        values = field[:, pl.ds(pl.multiple_of(k * chunk, chunk), chunk)].astype(BF16)
        total[...] += lax.dot_general(table_tile(table, k, wide), values, NT, preferred_element_type=F32)
        return carry

    lax.fori_loop(0, tiles, transform, 0)
    spec[...] = total[...].astype(BF16)


def mix_kernel(group, channels, forward, inverse, data, weight, out):
    rows = forward.shape[0]
    fan = weight.shape[1] // (2 * channels)
    row_wave = lax.broadcasted_iota(jnp.int32, (rows, 2 * channels), 0) % MX
    half = lax.broadcasted_iota(jnp.int32, (rows, 2 * channels), 1) // channels
    for g in range(group):
        modes = jnp.dot(forward[...], data[g], preferred_element_type=F32)
        twice = jnp.concatenate([modes, modes], axis=1)
        spread = jnp.concatenate(
            [jnp.where(row_wave == 2 * k + half, twice, 0.0).astype(BF16) for k in range(fan)], axis=1
        )
        prod = jnp.dot(spread, weight[g], preferred_element_type=F32)
        real, imag = prod[:MX], prod[MX:]
        mixed = jnp.concatenate(
            [
                real[:, :channels] - imag[:, channels:],
                real[:, channels:] + imag[:, :channels],
            ],
            axis=0,
        ).astype(BF16)
        out[g] = jnp.dot(inverse[...], mixed, preferred_element_type=F32).astype(BF16)


def layer_kernel(last, planes, wide, modes, table, field, up, down, out, *rest):
    channels = field.shape[0] // planes
    tile = table_tile(table, 0, wide)
    summed = out if not last else rest[0]
    summed[...] = field[...] + jnp.dot(modes[...], tile, preferred_element_type=F32)
    scale = math.sqrt(2.0 / math.pi)

    def one(p, carry):
        rows = pl.ds(pl.multiple_of(p * channels, channels), channels)
        values = summed[rows, :]
        v = jnp.dot(up[...], values.astype(BF16), preferred_element_type=F32)
        inner = v * (scale + (scale * 0.044715) * (v * v))
        halved = 0.5 * v
        active = (halved + halved * jnp.tanh(inner)).astype(BF16)
        values = values + jnp.dot(down[...], active, preferred_element_type=F32)
        out[rows, :] = values.astype(out.dtype)
        return carry

    lax.fori_loop(0, planes, one, 0)
    if not last:
        spec, total = rest

        @pl.when(pl.program_id(0) == 0)
        def _():
            total[...] = jnp.zeros_like(total)

        total[...] += lax.dot_general(tile, out[...].astype(BF16), NT, preferred_element_type=F32)

        @pl.when(pl.program_id(0) == pl.num_programs(0) - 1)
        def _():
            spec[...] = total[...].astype(BF16)


def pick_kernel(cap, per_plane, targets, field, send):
    channels, size = send.shape[2], send.shape[3]

    def one(d, carry):
        for i in range(cap):
            t = jnp.maximum(targets[d * cap + i], 0)
            rows = pl.ds(pl.multiple_of(t // per_plane * channels, channels), channels)
            cols = pl.ds(pl.multiple_of(t % per_plane * size, size), size)
            send[d, i] = field[rows, cols]
        return carry

    lax.fori_loop(0, send.shape[0], one, 0)


def decode_kernel(slot_of, got, kern, out):
    size = kern.shape[1]

    def one(b, carry):
        acc = None
        for k in range(NBR):
            p = b * NBR + k
            term = lax.dot_general(got[slot_of[p]], kern[p], NT, preferred_element_type=F32)
            acc = term if acc is None else acc + term
        out[:, pl.ds(pl.multiple_of(b * size, size), size)] = acc
        return carry

    lax.fori_loop(0, kern.shape[0] // NBR, one, 0)


def swap(values):
    return lax.all_to_all(values, "pen", split_axis=0, concat_axis=0, tiled=True)


def per_device(point_feat, pair_kernel, pair_owner, pair_block, spec_weight, mlp_up, mlp_down):
    devices = lax.axis_size("pen")
    pairs, size = pair_kernel.shape[0], pair_kernel.shape[1]
    channels = point_feat.shape[0]
    cap = 2 * pairs // devices
    planes = NX // devices
    plane_cells = NY * NZ
    per_plane = plane_cells // size
    here = spec_weight.shape[1]
    modes_all = MY * MZ
    hidden = mlp_up.shape[1]
    lines = planes * channels
    wide = 4
    table = plane_table(devices, size)
    forward, inverse = along_tables(devices)

    send, slot_of, targets = pl.pallas_call(
        functools.partial(encode_kernel, devices, cap),
        out_shape=(
            jax.ShapeDtypeStruct((devices, cap + 1, channels, size), BF16),
            jax.ShapeDtypeStruct((pairs,), jnp.int32),
            jax.ShapeDtypeStruct((devices * cap,), jnp.int32),
        ),
        in_specs=[SMEM, SMEM, VMEM, VMEM],
        out_specs=(VMEM, SMEM, SMEM),
        scratch_shapes=[pltpu.SMEM((devices,), jnp.int32)],
        name="encode",
    )(pair_owner[:, 0], pair_block, point_feat, pair_kernel)
    got = swap(send)
    wanted = got[:, cap, 0, :cap].astype(jnp.int32).reshape(devices * cap)

    field, spec = pl.pallas_call(
        functools.partial(gather_sums_kernel, cap, per_plane, wide),
        out_shape=(
            jax.ShapeDtypeStruct((lines, plane_cells), F32),
            jax.ShapeDtypeStruct((2 * modes_all, lines), BF16),
        ),
        in_specs=[SMEM, VMEM, VMEM],
        out_specs=(VMEM, VMEM),
        scratch_shapes=[pltpu.VMEM((2 * modes_all, lines), F32)],
        name="place",
    )(wanted, got, table)

    group = math.gcd(here, 4)
    first_mode = lax.axis_index("pen") * here
    wave_z = (first_mode + jnp.arange(here, dtype=jnp.int32)) % MZ
    scaling = jnp.where(wave_z == 0, 1.0, 2.0).astype(F32) / (NX * NY * NZ)
    for number in range(LAYERS):
        last = number == LAYERS - 1
        across = swap(spec.reshape(devices, 2 * here, lines))
        data = across.reshape(devices, 2, here, planes, channels).transpose(2, 0, 1, 3, 4)
        mixed = pl.pallas_call(
            functools.partial(mix_kernel, group, channels),
            out_shape=jax.ShapeDtypeStruct((here, 2 * NX, channels), BF16),
            grid=(here // group,),
            in_specs=[
                pl.BlockSpec((2 * MX, 2 * NX), lambda g: (0, 0)),
                pl.BlockSpec((2 * NX, 2 * MX), lambda g: (0, 0)),
                pl.BlockSpec((group, 2 * NX, channels), lambda g: (g, 0, 0)),
                pl.BlockSpec((group, MX * channels, 2 * channels), lambda g: (g, 0, 0)),
            ],
            out_specs=pl.BlockSpec((group, 2 * NX, channels), lambda g: (g, 0, 0)),
            name="mix",
        )(
            forward,
            inverse,
            data.reshape(here, 2 * NX, channels),
            spec_weight[number].reshape(here, MX * channels, 2 * channels),
        )
        mixed = mixed.astype(F32) * scaling[:, None, None]
        back = mixed.astype(BF16).reshape(here, devices, 2, planes, channels).transpose(1, 2, 0, 3, 4)
        modes = swap(back.reshape(devices, 2 * here, lines)).reshape(2 * modes_all, lines).T

        chunk = wide * size
        spec_shape = (2 * modes_all, lines)
        field_spec = pl.BlockSpec((lines, chunk), lambda k: (0, k))
        results = pl.pallas_call(
            functools.partial(layer_kernel, last, planes, wide),
            out_shape=(jax.ShapeDtypeStruct((lines, plane_cells), BF16 if last else F32),)
            + (() if last else (jax.ShapeDtypeStruct(spec_shape, BF16),)),
            grid=(plane_cells // chunk,),
            in_specs=[
                pl.BlockSpec((lines, 2 * modes_all), lambda k: (0, 0)),
                pl.BlockSpec((wide, 2 * modes_all, size), lambda k: (k, 0, 0)),
                field_spec,
                pl.BlockSpec((hidden, channels), lambda k: (0, 0)),
                pl.BlockSpec((channels, hidden), lambda k: (0, 0)),
            ],
            out_specs=(field_spec,) + (() if last else (pl.BlockSpec(spec_shape, lambda k: (0, 0)),)),
            scratch_shapes=[pltpu.VMEM((lines, chunk) if last else spec_shape, F32)],
            name="layer",
        )(modes, table, field, mlp_up[number], mlp_down[number])
        if last:
            field = results[0]
        else:
            field, spec = results

    picked = pl.pallas_call(
        functools.partial(pick_kernel, cap, per_plane),
        out_shape=jax.ShapeDtypeStruct((devices, cap, channels, size), BF16),
        in_specs=[SMEM, VMEM],
        out_specs=VMEM,
        name="pick",
    )(wanted, field)
    fetched = swap(picked).reshape(devices * cap, channels, size)
    return pl.pallas_call(
        decode_kernel,
        out_shape=jax.ShapeDtypeStruct((channels, pairs // NBR * size), F32),
        in_specs=[SMEM, VMEM, VMEM],
        out_specs=VMEM,
        name="decode",
    )(slot_of, fetched, pair_kernel)


def solution(mesh):
    in_specs = (
        P(None, ("groups", "pen")),
        P(("groups", "pen"), None, None),
        P(("groups", "pen"), None),
        P(("groups", "pen")),
        P(None, "pen", None, None, None),
        P(),
        P(),
    )
    out_specs = P(None, ("groups", "pen"))
    return jax.shard_map(
        per_device, mesh=mesh, in_specs=in_specs, out_specs=out_specs, check_vma=False
    )
```

time: 660 us -> 322 us (0.49); the launches traced: 649 us -> 322 us
  local copies, waits for them, and re-layouts: 215 us -> 19.5 us
  matrix products: 175 us -> 0 us
  Pallas kernels: 0 us -> 121 us
  other arithmetic: 68.3 us -> 9.63 us
  blocking collectives: 31.4 us -> 70.8 us
  waiting for transfers between devices: 108 us -> 72.6 us
  starting transfers between devices: 51.2 us -> 28.3 us
    dot_general x32 -> x0, matrix products: 175 us -> none  [the longest x2 50.8 us: channel_mlp(): jnp.dot(weight_down, active, preferred_element_type=jnp.float32)]
    pallas_call x0 -> x8, Pallas kernels: none -> 121 us  [the longest x2 72.6 us: per_device(): pl.pallas_call(functools.partial(layer_kernel, last, planes, wide), out_s...]
    reshape x10 -> x8, local copies, waits for them, and re-layouts: 58.1 us -> 6.45 us  [the longest x2 2.82 us: per_device(): back.reshape(devices, 2 * here, lines)]
    all_to_all x1 -> x2, blocking collectives: 31.4 us -> 70.8 us  [swap(): lax.all_to_all(values, 'pen', split_axis=0, concat_axis=0, tiled=True)]
    unnamed x38 -> x16, local copies, waits for them, and re-layouts: 38.6 us -> 2.13 us
    all_to_all x6 -> x4, waiting for transfers between devices: 108 us -> 72.6 us  [swap(): lax.all_to_all(values, 'pen', split_axis=0, concat_axis=0, tiled=True)]
    mul x2 -> x0, local copies, waits for them, and re-layouts: 24.3 us -> none  [yz_tables(): inverse_table = forward_table * jnp.repeat(scaling, 2)[None, :]]
    all_to_all x6 -> x4, starting transfers between devices: 51.2 us -> 28.3 us  [swap(): lax.all_to_all(values, 'pen', split_axis=0, concat_axis=0, tiled=True)]
  transfers between devices with their start and end apart: 6 -> 4, of which waited for: 4 -> 4; matrix products, arithmetic and copies ran while one was open for 15% -> 5% of each run, Pallas kernels for 0% -> 0%
where the time goes in v1:
time: 322 us
  Pallas kernels  121 us (38%)
  waiting for transfers between devices  72.6 us (23%)
  blocking collectives  70.8 us (22%)
  starting transfers between devices  28.3 us (9%)
  local copies, waits for them, and re-layouts  19.5 us (6%)
  other arithmetic  9.63 us (3%)
    pallas_call x2, Pallas kernels, per_device(): pl.pallas_call(functools.partial(layer_kernel, last, planes, wide), out_s...  72.6 us
    all_to_all x4, waiting for transfers between devices, swap(): lax.all_to_all(values, 'pen', split_axis=0, concat_axis=0, tiled=True)  72.6 us
    all_to_all x2, blocking collectives, swap(): lax.all_to_all(values, 'pen', split_axis=0, concat_axis=0, tiled=True)  70.8 us
    all_to_all x4, starting transfers between devices, swap(): lax.all_to_all(values, 'pen', split_axis=0, concat_axis=0, tiled=True)  28.3 us
    pallas_call x2, Pallas kernels, per_device(): pl.pallas_call(functools.partial(mix_kernel, group, channels), out_shape=...  18.6 us
    pallas_call x1, Pallas kernels, per_device(): pl.pallas_call(functools.partial(gather_sums_kernel, cap, per_plane, wide...  12.3 us
    slice x1, local copies, waits for them, and re-layouts, per_device(): spec_weight[number].reshape(here, MX * channels, 2 * channels)  6.89 us
    pallas_call x1, Pallas kernels, per_device(): pl.pallas_call(functools.partial(encode_kernel, devices, cap), out_shape=...  6.49 us
  transfers between devices with their start and end apart: 4, of which 4 were waited for; matrix products, arithmetic and copies ran while one was open for 5% of the time, Pallas kernels for 0%

profile of v1, /device:TPU:1, one launch (start us, length us, event | category | flops | bytes accessed | tf_op | source)
XLA Modules:
  0.0 321.6 jit_solution(13248157472820205222)
XLA Ops:
  0.0 0.0 copy-start.2
  0.0 0.0 copy-start.3
  0.0 0.0 copy-start.4
  0.0 6.5 %encode.1 = (bf16[16,9,64,128]{3,2,1,0:T(8,128)(2,1)}, s32[64]{0:T(128)}, s32[128]{0:T(128)}) custom-call(s32[64]{0:T(128)} %bitcast.51, s32[64]{0:T(128)} %block.1, bf16[64,2048]{1,0:T(8,128)(2,1)} %feat.1, bf16[64,128,128]{2,1,0:T(8,128)(2,1)} %kern.3), custom_call_target="tpu_custom_call" | custom-call | tf_op jit(solution)/shard_map/encode/pallas_call | solution.py:239
  6.5 7.4 %all-to-all-start = ((bf16[16,9,64,128]{3,2,1,0:T(8,128)(2,1)}), bf16[16,9,64,128]{3,2,1,0:T(8,128)(2,1)S(1)}, u32[]{:S(2)}, u32[]{:S(2)}) async-start(bf16[16,9,64,128]{3,2,1,0:T(8,128)(2,1)} %get-tuple-element.16), calls=%async_computation | async-start | bytes 4718592 | tf_op jit(solution)/shard_map/all_to_all | solution.py:220
  13.9 0.0 copy-done.1
  13.9 0.0 copy-done.2
  13.9 0.0 copy-done.3
  13.9 0.0 copy-done.4
  13.9 6.4 %subtract_convert_fusion.table = bf16[32,512,128]{2,1,0:T(8,128)(2,1)} fusion(f32[32,512]{1,0:T(8,128)S(1)} %copy-done.4, f32[512,128]{1,0:T(8,128)S(1)} %copy-done.2, f32[32,512]{1,0:T(8,128)S(1)} %copy-done.3, f32[512,128]{1,0:T(8,128)S(1)} %copy-done.1), kind=kLoop, calls=%fused_computation | loop fusion | flops 8388608 | bytes 4849664 | tf_op jit(solution)/shard_map/convert_element_type | solution.py:42
  20.3 39.6 %all-to-all-done.got = bf16[16,9,64,128]{3,2,1,0:T(8,128)(2,1)S(1)} async-done(((bf16[16,9,64,128]{3,2,1,0:T(8,128)(2,1)}), bf16[16,9,64,128]{3,2,1,0:T(8,128)(2,1)S(1)}, u32[]{:S(2)}, u32[]{:S(2)}) %all-to-all-start) | async-done | bytes 2359328 | tf_op jit(solution)/shard_map/all_to_all | solution.py:220
  60.0 0.0 copy-start
  60.0 0.8 reshape.78.targets
  60.8 0.6 copy-done
  61.5 12.3 %place.1 = (f32[512,4096]{1,0:T(8,128)}, bf16[512,512]{1,0:T(8,128)(2,1)}) custom-call(s32[128]{0:T(128)} %reshape.78.targets, bf16[16,9,64,128]{3,2,1,0:T(8,128)(2,1)} %copy-done, bf16[32,512,128]{2,1,0:T(8,128)(2,1)} %subtract_convert_fusion.table), custom_call_target="tpu_custom_call" | custom-call | tf_op jit(solution)/shard_map/place/pallas_call | solution.py:254
  73.8 12.0 %all-to-all-start.1 = ((bf16[16,32,512]{2,1,0:T(8,128)(2,1)}), bf16[16,32,512]{2,1,0:T(8,128)(2,1)S(1)}, u32[]{:S(2)}, u32[]{:S(2)}) async-start(bf16[16,32,512]{2,1,0:T(8,128)(2,1)} %bitcast.47), calls=%async_computation.1 | async-start | bytes 1048576 | tf_op jit(solution)/shard_map/all_to_all | solution.py:220
  85.8 6.9 %fusion.3 = (bf16[1,16,16,64,128]{4,3,2,1,0:T(8,128)(2,1)}, bf16[1,16,16,64,128]{4,3,2,1,0:T(8,128)(2,1)}) fusion(bf16[2,16,16,64,128]{4,3,2,1,0:T(8,128)(2,1)} %param.17), kind=kLoop, calls=%fused_computation.15 | loop fusion | bytes 16777216 | tf_op jit(solution)/shard_map/slice | solution.py:290
  92.7 7.1 %all-to-all-done.1 = bf16[16,32,512]{2,1,0:T(8,128)(2,1)S(1)} async-done(((bf16[16,32,512]{2,1,0:T(8,128)(2,1)}), bf16[16,32,512]{2,1,0:T(8,128)(2,1)S(1)}, u32[]{:S(2)}, u32[]{:S(2)}) %all-to-all-start.1) | async-done | bytes 524320 | tf_op jit(solution)/shard_map/all_to_all | solution.py:220
  99.8 0.5 reshape.66
  100.3 1.3 copy.17
  101.6 9.3 %mix.2 = bf16[16,256,64]{2,1,0:T(8,128)(2,1)} custom-call(bf16[32,256]{1,0:T(8,128)(2,1)} %constant.43.clone.forward, bf16[256,32]{1,0:T(8,128)(2,1)} %constant.44.clone.inverse, bf16[16,256,64]{2,1,0:T(8,128)(2,1)} %bitcast.36, bf16[16,1024,128]{2,1,0:T(8,128)(2,1)} %bitcast.33), custom_call_target="tpu_custom_call" | custom-call | tf_op jit(solution)/shard_map/mix/pallas_call | solution.py:274
  111.0 0.0 copy-start.6
  111.0 1.6 multiply_convert_fusion.1
  112.6 0.3 copy.30
  112.8 1.4 reshape.69
  114.3 4.4 %all-to-all-start.2 = ((bf16[16,32,512]{2,1,0:T(8,128)(2,1)}), bf16[16,32,512]{2,1,0:T(8,128)(2,1)S(1)}, u32[]{:S(2)}, u32[]{:S(2)}) async-start(bf16[16,32,512]{2,1,0:T(8,128)(2,1)} %reshape.69), calls=%async_computation.2 | async-start | bytes 1048576 | tf_op jit(solution)/shard_map/all_to_all | solution.py:220
  118.7 0.0 copy-done.5
  118.7 0.7 copy.25
  119.5 0.0 copy-done.6
  119.5 0.6 slice_bitcast_fusion
  120.1 12.6 %all-to-all-done.2 = bf16[16,32,512]{2,1,0:T(8,128)(2,1)S(1)} async-done(((bf16[16,32,512]{2,1,0:T(8,128)(2,1)}), bf16[16,32,512]{2,1,0:T(8,128)(2,1)S(1)}, u32[]{:S(2)}, u32[]{:S(2)}) %all-to-all-start.2) | async-done | bytes 524320 | tf_op jit(solution)/shard_map/all_to_all | solution.py:220
  132.7 1.0 copy.19
  133.7 38.5 %layer.2 = (f32[512,4096]{1,0:T(8,128)}, bf16[512,512]{1,0:T(8,128)(2,1)}) custom-call(bf16[512,512]{1,0:T(8,128)(2,1)} %bitcast.43, bf16[32,512,128]{2,1,0:T(8,128)(2,1)} %subtract_convert_fusion.table, f32[512,4096]{1,0:T(8,128)} %get-tuple-element.22.field, bf16[256,64]{1,0:T(8,128)(2,1)} %bitcast.49, bf16[64,256]{1,0:T(8,128)(2,1)} %get-tuple-element.28.down), custom_call_target="tpu_custom_call" | custom-call | tf_op jit(solution)/shard_map/layer/pallas_call | solution.py:299
  172.2 18.4 %all_to_all.30 = bf16[16,32,512]{2,1,0:T(8,128)(2,1)S(1)} all-to-all(bf16[16,32,512]{2,1,0:T(8,128)(2,1)} %bitcast.48), channel_id=1, replica_groups=mesh['groups'=2,'pen'=16] {'pen'}, dimensions={0} | all-to-all | bytes 1048576 | tf_op jit(solution)/shard_map/all_to_all | solution.py:220
  190.6 0.5 reshape.72
  191.2 1.3 copy.21
  192.4 9.3 %mix.3 = bf16[16,256,64]{2,1,0:T(8,128)(2,1)} custom-call(bf16[32,256]{1,0:T(8,128)(2,1)} %constant.43.clone.forward, bf16[256,32]{1,0:T(8,128)(2,1)} %constant.44.clone.inverse, bf16[16,256,64]{2,1,0:T(8,128)(2,1)} %bitcast.35, bf16[16,1024,128]{2,1,0:T(8,128)(2,1)} %bitcast.32), custom_call_target="tpu_custom_call" | custom-call | tf_op jit(solution)/shard_map/mix/pallas_call | solution.py:274
  201.7 1.6 multiply_convert_fusion
  203.3 0.3 copy.29
  203.6 1.4 reshape.75
  205.0 4.4 %all-to-all-start.4 = ((bf16[16,32,512]{2,1,0:T(8,128)(2,1)}), bf16[16,32,512]{2,1,0:T(8,128)(2,1)S(1)}, u32[]{:S(2)}, u32[]{:S(2)}) async-start(bf16[16,32,512]{2,1,0:T(8,128)(2,1)} %reshape.75), calls=%async_computation.4 | async-start | bytes 1048576 | tf_op jit(solution)/shard_map/all_to_all | solution.py:220
  209.4 0.7 copy.26
  210.2 13.3 %all-to-all-done.4 = bf16[16,32,512]{2,1,0:T(8,128)(2,1)S(1)} async-done(((bf16[16,32,512]{2,1,0:T(8,128)(2,1)}), bf16[16,32,512]{2,1,0:T(8,128)(2,1)S(1)}, u32[]{:S(2)}, u32[]{:S(2)}) %all-to-all-start.4) | async-done | bytes 524320 | tf_op jit(solution)/shard_map/all_to_all | solution.py:220
  223.4 1.0 copy.23
  224.4 34.2 %layer.3.field = bf16[512,4096]{1,0:T(8,128)(2,1)} custom-call(bf16[512,512]{1,0:T(8,128)(2,1)} %bitcast.44, bf16[32,512,128]{2,1,0:T(8,128)(2,1)} %subtract_convert_fusion.table, f32[512,4096]{1,0:T(8,128)} %get-tuple-element.24.field, bf16[256,64]{1,0:T(8,128)(2,1)} %bitcast.50, bf16[64,256]{1,0:T(8,128)(2,1)} %get-tuple-element.27.down), custom_call_target="tpu_custom_call" | custom-call | tf_op jit(solution)/shard_map/layer/pallas_call | solution.py:299
  258.6 4.4 %pick.1 = bf16[16,8,64,128]{3,2,1,0:T(8,128)(2,1)} custom-call(s32[128]{0:T(128)} %reshape.78.targets, bf16[512,4096]{1,0:T(8,128)(2,1)} %layer.3.field), custom_call_target="tpu_custom_call" | custom-call | tf_op jit(solution)/shard_map/pick/pallas_call | solution.py:320
  263.0 52.4 %all_to_all.31 = bf16[16,8,64,128]{3,2,1,0:T(8,128)(2,1)} all-to-all(bf16[16,8,64,128]{3,2,1,0:T(8,128)(2,1)} %pick.1), channel_id=1, replica_groups=mesh['groups'=2,'pen'=16] {'pen'}, dimensions={0} | all-to-all | bytes 4194304 | tf_op jit(solution)/shard_map/all_to_all | solution.py:220
  315.4 6.2 %decode.1 = f32[64,2048]{1,0:T(8,128)} custom-call(s32[64]{0:T(128)} %get-tuple-element.15.slot_of, bf16[128,64,128]{2,1,0:T(8,128)(2,1)} %bitcast.34, bf16[64,128,128]{2,1,0:T(8,128)(2,1)} %kern.3), custom_call_target="tpu_custom_call" | custom-call | tf_op jit(solution)/shard_map/decode/pallas_call | solution.py:328
  (5 shorter events, 0.1 us)
Async XLA Ops:
  0.0 13.9 %copy-start.1 = (f32[512,128]{1,0:T(8,128)S(1)}, f32[512,128]{1,0:T(8,128)}, u32[]{:S(2)}) copy-start(f32[512,128]{1,0:T(8,128)} %constant.39.clone) | copy-start | bytes 786436
  0.0 13.9 %copy-start.2 = (f32[512,128]{1,0:T(8,128)S(1)}, f32[512,128]{1,0:T(8,128)}, u32[]{:S(2)}) copy-start(f32[512,128]{1,0:T(8,128)} %constant.40.clone) | copy-start | bytes 786436
  0.0 13.9 %copy-start.3 = (f32[32,512]{1,0:T(8,128)S(1)}, f32[32,512]{1,0:T(8,128)}, u32[]{:S(2)}) copy-start(f32[32,512]{1,0:T(8,128)} %constant.41.clone) | copy-start | bytes 196612
  0.0 13.9 %copy-start.4 = (f32[32,512]{1,0:T(8,128)S(1)}, f32[32,512]{1,0:T(8,128)}, u32[]{:S(2)}) copy-start(f32[32,512]{1,0:T(8,128)} %constant.42.clone) | copy-start | bytes 196612
  6.5 53.5 %all-to-all-start = ((bf16[16,9,64,128]{3,2,1,0:T(8,128)(2,1)}), bf16[16,9,64,128]{3,2,1,0:T(8,128)(2,1)S(1)}, u32[]{:S(2)}, u32[]{:S(2)}) async-start(bf16[16,9,64,128]{3,2,1,0:T(8,128)(2,1)} %get-tuple-element.16), calls=%async_computation | async-start | bytes 4718592 | tf_op jit(solution)/shard_map/all_to_all | solution.py:220
  60.0 1.5 copy-start
  73.8 26.0 %all-to-all-start.1 = ((bf16[16,32,512]{2,1,0:T(8,128)(2,1)}), bf16[16,32,512]{2,1,0:T(8,128)(2,1)S(1)}, u32[]{:S(2)}, u32[]{:S(2)}) async-start(bf16[16,32,512]{2,1,0:T(8,128)(2,1)} %bitcast.47), calls=%async_computation.1 | async-start | bytes 1048576 | tf_op jit(solution)/shard_map/all_to_all | solution.py:220
  111.0 7.7 %copy-start.5 = (bf16[2,256,64]{1,2,0:T(8,128)(2,1)S(1)}, bf16[2,256,64]{1,2,0:T(8,128)(2,1)}, u32[]{:S(2)}) copy-start(bf16[2,256,64]{1,2,0:T(8,128)(2,1)} %param.18) | copy-start | bytes 196612
  111.0 8.5 %copy-start.6 = (bf16[2,64,256]{2,1,0:T(8,128)(2,1)S(1)}, bf16[2,64,256]{2,1,0:T(8,128)(2,1)}, u32[]{:S(2)}) copy-start(bf16[2,64,256]{2,1,0:T(8,128)(2,1)} %param.19) | copy-start | bytes 196612
  114.3 18.4 %all-to-all-start.2 = ((bf16[16,32,512]{2,1,0:T(8,128)(2,1)}), bf16[16,32,512]{2,1,0:T(8,128)(2,1)S(1)}, u32[]{:S(2)}, u32[]{:S(2)}) async-start(bf16[16,32,512]{2,1,0:T(8,128)(2,1)} %reshape.69), calls=%async_computation.2 | async-start | bytes 1048576 | tf_op jit(solution)/shard_map/all_to_all | solution.py:220
  205.0 18.4 %all-to-all-start.4 = ((bf16[16,32,512]{2,1,0:T(8,128)(2,1)}), bf16[16,32,512]{2,1,0:T(8,128)(2,1)S(1)}, u32[]{:S(2)}, u32[]{:S(2)}) async-start(bf16[16,32,512]{2,1,0:T(8,128)(2,1)} %reshape.75), calls=%async_computation.4 | async-start | bytes 1048576 | tf_op jit(solution)/shard_map/all_to_all | solution.py:220

commit v2 on v1

--- a/solution.py
+++ b/solution.py
@@ -51,7 +51,9 @@
     to_real = np.stack([cos, sin], axis=2)
     to_imag = np.stack([-sin, cos], axis=2)
     forward = np.concatenate([to_real, to_imag], axis=0).reshape(2 * MX, 2 * NX)
-    return jnp.asarray(forward, BF16), jnp.asarray(forward.T, BF16)
+    high = forward.astype(jnp.bfloat16).astype(np.float64)
+    both = np.concatenate([high, forward - high], axis=0)
+    return jnp.asarray(both, BF16), jnp.asarray(both.T, BF16)
 
 
 def encode_kernel(devices, cap, owner, block, feat, kern, send, slot_of, targets, count):
@@ -131,27 +133,39 @@
     spec[...] = total[...].astype(BF16)
 
 
-def mix_kernel(group, channels, forward, inverse, data, weight, out):
-    rows = forward.shape[0]
-    fan = weight.shape[1] // (2 * channels)
-    row_wave = lax.broadcasted_iota(jnp.int32, (rows, 2 * channels), 0) % MX
-    half = lax.broadcasted_iota(jnp.int32, (rows, 2 * channels), 1) // channels
-    for g in range(group):
-        modes = jnp.dot(forward[...], data[g], preferred_element_type=F32)
-        twice = jnp.concatenate([modes, modes], axis=1)
-        spread = jnp.concatenate(
-            [jnp.where(row_wave == 2 * k + half, twice, 0.0).astype(BF16) for k in range(fan)], axis=1
-        )
-        prod = jnp.dot(spread, weight[g], preferred_element_type=F32)
-        real, imag = prod[:MX], prod[MX:]
-        mixed = jnp.concatenate(
-            [
-                real[:, :channels] - imag[:, channels:],
-                real[:, channels:] + imag[:, :channels],
-            ],
-            axis=0,
-        ).astype(BF16)
-        out[g] = jnp.dot(inverse[...], mixed, preferred_element_type=F32).astype(BF16)
+def mix_kernel(channels, forward, inverse, data, weight, scaling, out, mixed):
+    rows = 2 * MX
+    here, fan = weight.shape[0], weight.shape[1] // (2 * channels)
+    width = 2 * channels
+    row_wave = lax.broadcasted_iota(jnp.int32, (rows, width), 0) % MX
+    half = lax.broadcasted_iota(jnp.int32, (rows, width), 1) // channels
+    left = half == 0
+    modes = jnp.dot(forward[...], data[...], preferred_element_type=F32)
+    modes = modes[:rows] + modes[rows:]
+    for pair in range(here // 2):
+        own = modes[:, pair * width : (pair + 1) * width]
+        other = pltpu.roll(own, channels, 1)
+        halves = []
+        for k in range(2):
+            twice = jnp.where(left, own, other) if k == 0 else jnp.where(left, other, own)
+            spread = jnp.concatenate(
+                [jnp.where(row_wave == 2 * f + half, twice, 0.0).astype(BF16) for f in range(fan)], axis=1
+            )
+            prod = jnp.dot(spread, weight[2 * pair + k], preferred_element_type=F32)
+            real, imag = prod[:MX], prod[MX:]
+            real_turned = pltpu.roll(real, channels, 1)
+            imag_turned = pltpu.roll(imag, channels, 1)
+            if k == 0:
+                halves.append((real - imag_turned, real_turned + imag))
+            else:
+                halves.append((real_turned - imag, real + imag_turned))
+        (real_a, imag_a), (real_b, imag_b) = halves
+        top = left[:MX]
+        both = jnp.concatenate([jnp.where(top, real_a, real_b), jnp.where(top, imag_a, imag_b)], axis=0)
+        both = (both * scaling[:, pair * width : (pair + 1) * width]).astype(BF16)
+        mixed[0:rows, pair * width : (pair + 1) * width] = both
+        mixed[rows : 2 * rows, pair * width : (pair + 1) * width] = both
+    out[...] = jnp.dot(inverse[...], mixed[...], preferred_element_type=F32).astype(BF16)
 
 
 def layer_kernel(last, planes, wide, modes, table, field, up, down, out, *rest):
@@ -160,19 +174,23 @@
     summed = out if not last else rest[0]
     summed[...] = field[...] + jnp.dot(modes[...], tile, preferred_element_type=F32)
     scale = math.sqrt(2.0 / math.pi)
-
-    def one(p, carry):
-        rows = pl.ds(pl.multiple_of(p * channels, channels), channels)
-        values = summed[rows, :]
-        v = jnp.dot(up[...], values.astype(BF16), preferred_element_type=F32)
-        inner = v * (scale + (scale * 0.044715) * (v * v))
-        halved = 0.5 * v
-        active = (halved + halved * jnp.tanh(inner)).astype(BF16)
-        values = values + jnp.dot(down[...], active, preferred_element_type=F32)
+    down_half = (down[...].astype(F32) * 0.5).astype(BF16)
+
+    def raise_up(p):
+        values = summed[p * channels : (p + 1) * channels, :]
+        return jnp.dot(up[...], values.astype(BF16), preferred_element_type=F32).astype(BF16)
+
+    ahead = raise_up(0)
+    for p in range(planes):
+        v = ahead
+        if p + 1 < planes:
+            ahead = raise_up(p + 1)
+        rows = slice(p * channels, (p + 1) * channels)
+        turn = jnp.tanh(v * (BF16(scale) + BF16(scale * 0.044715) * (v * v)))
+        active = v + v * turn
+        values = summed[rows, :] + jnp.dot(down_half, active, preferred_element_type=F32)
         out[rows, :] = values.astype(out.dtype)
-        return carry
-
-    lax.fori_loop(0, planes, one, 0)
+
     if not last:
         spec, total = rest
 
@@ -263,35 +281,33 @@
         name="place",
     )(wanted, got, table)
 
-    group = math.gcd(here, 4)
     first_mode = lax.axis_index("pen") * here
-    wave_z = (first_mode + jnp.arange(here, dtype=jnp.int32)) % MZ
-    scaling = jnp.where(wave_z == 0, 1.0, 2.0).astype(F32) / (NX * NY * NZ)
+    wave_z = (first_mode + jnp.arange(here * channels, dtype=jnp.int32) // channels) % MZ
+    scaling = (jnp.where(wave_z == 0, 1.0, 2.0).astype(F32) / (NX * NY * NZ))[None, :]
+    weights = spec_weight.reshape(LAYERS * here, MX * channels, 2 * channels)
+    whole = lambda shape: pl.BlockSpec(shape, lambda g: (0,) * len(shape))
     for number in range(LAYERS):
         last = number == LAYERS - 1
         across = swap(spec.reshape(devices, 2 * here, lines))
-        data = across.reshape(devices, 2, here, planes, channels).transpose(2, 0, 1, 3, 4)
+        data = across.reshape(devices, 2, here, planes, channels).transpose(0, 1, 3, 2, 4)
         mixed = pl.pallas_call(
-            functools.partial(mix_kernel, group, channels),
-            out_shape=jax.ShapeDtypeStruct((here, 2 * NX, channels), BF16),
-            grid=(here // group,),
+            functools.partial(mix_kernel, channels),
+            out_shape=jax.ShapeDtypeStruct((2 * NX, here * channels), BF16),
+            grid=(1,),
             in_specs=[
-                pl.BlockSpec((2 * MX, 2 * NX), lambda g: (0, 0)),
-                pl.BlockSpec((2 * NX, 2 * MX), lambda g: (0, 0)),
-                pl.BlockSpec((group, 2 * NX, channels), lambda g: (g, 0, 0)),
-                pl.BlockSpec((group, MX * channels, 2 * channels), lambda g: (g, 0, 0)),
+                whole((4 * MX, 2 * NX)),
+                whole((2 * NX, 4 * MX)),
+                whole((2 * NX, here * channels)),
+                pl.BlockSpec((here, MX * channels, 2 * channels), lambda g, n=number: (n, 0, 0)),
+                whole((1, here * channels)),
             ],
-            out_specs=pl.BlockSpec((group, 2 * NX, channels), lambda g: (g, 0, 0)),
+            out_specs=whole((2 * NX, here * channels)),
+            scratch_shapes=[pltpu.VMEM((4 * MX, here * channels), BF16)],
             name="mix",
-        )(
-            forward,
-            inverse,
-            data.reshape(here, 2 * NX, channels),
-            spec_weight[number].reshape(here, MX * channels, 2 * channels),
-        )
-        mixed = mixed.astype(F32) * scaling[:, None, None]
-        back = mixed.astype(BF16).reshape(here, devices, 2, planes, channels).transpose(1, 2, 0, 3, 4)
-        modes = swap(back.reshape(devices, 2 * here, lines)).reshape(2 * modes_all, lines).T
+        )(forward, inverse, data.reshape(2 * NX, here * channels), weights, scaling)
+        modes = swap(mixed.reshape(devices, 2 * planes, here * channels))
+        modes = modes.reshape(devices, 2, planes, here, channels).transpose(0, 1, 3, 2, 4)
+        modes = modes.reshape(2 * modes_all, lines).T
 
         chunk = wide * size
         spec_shape = (2 * modes_all, lines)

time: 322 us -> 272 us (0.84)
  Pallas kernels: 121 us -> 71.6 us
  local copies, waits for them, and re-layouts: 19.5 us -> 13.1 us
  waiting for transfers between devices: 72.6 us -> 77.6 us
    pallas_call x2, Pallas kernels: 72.6 us -> 33.6 us  [per_device(): pl.pallas_call(functools.partial(layer_kernel, last, planes, wide), out_s...]
    pallas_call x2, Pallas kernels: 18.6 us -> 8.74 us  [per_device(): pl.pallas_call(functools.partial(mix_kernel, channels), out_shape=jax.Sha...]
    slice x1 -> x0, local copies, waits for them, and re-layouts: 6.89 us -> none  [per_device(): spec_weight[number].reshape(here, MX * channels, 2 * channels)]
    all_to_all x4, waiting for transfers between devices: 72.6 us -> 77.6 us  [swap(): lax.all_to_all(values, 'pen', split_axis=0, concat_axis=0, tiled=True)]
    reshape x8 -> x10, local copies, waits for them, and re-layouts: 6.45 us -> 8.62 us  [the longest x4 3.23 us: per_device(): modes = modes.reshape(2 * modes_all, lines).T]
  transfers between devices with their start and end apart: 4 -> 4, of which waited for: 4 -> 4; matrix products, arithmetic and copies ran while one was open for 5% -> 4% of each run, Pallas kernels for 0% -> 0%
where the time goes in v2:
time: 272 us; the launch traced here: 270 us
  waiting for transfers between devices  77.6 us (29%)
  Pallas kernels  71.6 us (26%)
  blocking collectives  70.8 us (26%)
  starting transfers between devices  28.1 us (10%)
  local copies, waits for them, and re-layouts  13.1 us (5%)
  other arithmetic  8.39 us (3%)
    all_to_all x4, waiting for transfers between devices, swap(): lax.all_to_all(values, 'pen', split_axis=0, concat_axis=0, tiled=True)  77.6 us
    all_to_all x2, blocking collectives, swap(): lax.all_to_all(values, 'pen', split_axis=0, concat_axis=0, tiled=True)  70.8 us
    pallas_call x2, Pallas kernels, per_device(): pl.pallas_call(functools.partial(layer_kernel, last, planes, wide), out_s...  33.6 us
    all_to_all x4, starting transfers between devices, swap(): lax.all_to_all(values, 'pen', split_axis=0, concat_axis=0, tiled=True)  28.1 us
    pallas_call x1, Pallas kernels, per_device(): pl.pallas_call(functools.partial(gather_sums_kernel, cap, per_plane, wide...  12.3 us
    pallas_call x2, Pallas kernels, per_device(): pl.pallas_call(functools.partial(mix_kernel, channels), out_shape=jax.Sha...  8.74 us
    convert_element_type x1, other arithmetic, plane_table(): (cos0[None] * cos_k[:, :, None] - sin0[None] * sin_k[:, :, None]).astype(...  7.74 us
    pallas_call x1, Pallas kernels, per_device(): pl.pallas_call(functools.partial(encode_kernel, devices, cap), out_shape=...  6.43 us
  transfers between devices with their start and end apart: 4, of which 4 were waited for; matrix products, arithmetic and copies ran while one was open for 4% of the time, Pallas kernels for 0%

profile of v2, /device:TPU:1, one launch (start us, length us, event | category | flops | bytes accessed | tf_op | source)
XLA Modules:
  0.0 269.7 jit_solution(15141781126009116999)
XLA Ops:
  0.0 6.4 %encode.1 = (bf16[16,9,64,128]{3,2,1,0:T(8,128)(2,1)}, s32[64]{0:T(128)}, s32[128]{0:T(128)}) custom-call(s32[64]{0:T(128)} %bitcast.42, s32[64]{0:T(128)} %block.1, bf16[64,2048]{1,0:T(8,128)(2,1)} %feat.1, bf16[64,128,128]{2,1,0:T(8,128)(2,1)} %kern.3), custom_call_target="tpu_custom_call" | custom-call | tf_op jit(solution)/shard_map/encode/pallas_call | solution.py:257
  6.4 7.3 %all-to-all-start = ((bf16[16,9,64,128]{3,2,1,0:T(8,128)(2,1)}), bf16[16,9,64,128]{3,2,1,0:T(8,128)(2,1)S(1)}, u32[]{:S(2)}, u32[]{:S(2)}) async-start(bf16[16,9,64,128]{3,2,1,0:T(8,128)(2,1)} %get-tuple-element.16), calls=%async_computation | async-start | bytes 4718592 | tf_op jit(solution)/shard_map/all_to_all | solution.py:238
  13.8 7.7 %subtract_convert_fusion.table = bf16[32,512,128]{2,1,0:T(8,128)(2,1)} fusion(f32[32,512]{1,0:T(8,128)} %constant.59.clone, f32[512,128]{1,0:T(8,128)} %constant.57.clone, f32[32,512]{1,0:T(8,128)} %constant.58.clone, f32[512,128]{1,0:T(8,128)} %constant.56.clone), kind=kLoop, calls=%fused_computation | loop fusion | flops 8388608 | bytes 4849664 | tf_op jit(solution)/shard_map/convert_element_type | solution.py:42
  21.5 38.4 %all-to-all-done.got = bf16[16,9,64,128]{3,2,1,0:T(8,128)(2,1)S(1)} async-done(((bf16[16,9,64,128]{3,2,1,0:T(8,128)(2,1)}), bf16[16,9,64,128]{3,2,1,0:T(8,128)(2,1)S(1)}, u32[]{:S(2)}, u32[]{:S(2)}) %all-to-all-start) | async-done | bytes 2359328 | tf_op jit(solution)/shard_map/all_to_all | solution.py:238
  59.9 0.0 copy-start
  59.9 0.8 reshape.143.targets
  60.7 0.6 copy-done
  61.3 12.3 %place.1 = (f32[512,4096]{1,0:T(8,128)}, bf16[512,512]{1,0:T(8,128)(2,1)}) custom-call(s32[128]{0:T(128)} %reshape.143.targets, bf16[16,9,64,128]{3,2,1,0:T(8,128)(2,1)} %copy-done, bf16[32,512,128]{2,1,0:T(8,128)(2,1)} %subtract_convert_fusion.table), custom_call_target="tpu_custom_call" | custom-call | tf_op jit(solution)/shard_map/place/pallas_call | solution.py:272
  73.6 0.0 copy-start.1
  73.6 0.0 copy-start.2
  73.6 11.9 %all-to-all-start.1 = ((bf16[16,32,512]{2,1,0:T(8,128)(2,1)}), bf16[16,32,512]{2,1,0:T(8,128)(2,1)S(1)}, u32[]{:S(2)}, u32[]{:S(2)}) async-start(bf16[16,32,512]{2,1,0:T(8,128)(2,1)} %bitcast.38), calls=%async_computation.1 | async-start | bytes 1048576 | tf_op jit(solution)/shard_map/all_to_all | solution.py:238
  85.4 0.6 fusion.2.scaling
  86.1 13.4 %all-to-all-done.1 = bf16[16,32,512]{2,1,0:T(8,128)(2,1)S(1)} async-done(((bf16[16,32,512]{2,1,0:T(8,128)(2,1)}), bf16[16,32,512]{2,1,0:T(8,128)(2,1)S(1)}, u32[]{:S(2)}, u32[]{:S(2)}) %all-to-all-start.1) | async-done | bytes 524320 | tf_op jit(solution)/shard_map/all_to_all | solution.py:238
  99.4 0.5 reshape.130
  100.0 0.2 copy.16
  100.2 1.5 reshape.131.data
  101.7 4.4 %mix.2 = bf16[256,1024]{1,0:T(8,128)(2,1)} custom-call(bf16[64,256]{1,0:T(8,128)(2,1)} %constant.60.clone.forward, bf16[256,64]{1,0:T(8,128)(2,1)} %constant.61.clone.inverse, bf16[256,1024]{1,0:T(8,128)(2,1)} %reshape.131.data, bf16[32,1024,128]{2,1,0:T(8,128)(2,1)} %bitcast.27, f32[1,1024]{1,0:T(1,128)} %fusion.2.scaling), custom_call_target="tpu_custom_call" | custom-call | tf_op jit(solution)/shard_map/mix/pallas_call | solution.py:293
  106.1 4.4 %all-to-all-start.2 = ((bf16[16,16,1024]{2,1,0:T(8,128)(2,1)}), bf16[16,16,1024]{2,1,0:T(8,128)(2,1)S(1)}, u32[]{:S(2)}, u32[]{:S(2)}) async-start(bf16[16,16,1024]{2,1,0:T(8,128)(2,1)} %bitcast.34), calls=%async_computation.2 | async-start | bytes 1048576 | tf_op jit(solution)/shard_map/all_to_all | solution.py:238
  110.5 0.0 copy-done.1
  110.5 0.7 copy.24
  111.3 0.0 copy-done.2
  111.3 0.6 slice_bitcast_fusion
  111.9 12.6 %all-to-all-done.2 = bf16[16,16,1024]{2,1,0:T(8,128)(2,1)S(1)} async-done(((bf16[16,16,1024]{2,1,0:T(8,128)(2,1)}), bf16[16,16,1024]{2,1,0:T(8,128)(2,1)S(1)}, u32[]{:S(2)}, u32[]{:S(2)}) %all-to-all-start.2) | async-done | bytes 524320 | tf_op jit(solution)/shard_map/all_to_all | solution.py:238
  124.5 0.7 reshape.134
  125.2 0.3 copy.17
  125.5 0.6 reshape.135
  126.1 1.0 copy.18
  127.1 18.8 %layer.2 = (f32[512,4096]{1,0:T(8,128)}, bf16[512,512]{1,0:T(8,128)(2,1)}) custom-call(bf16[512,512]{1,0:T(8,128)(2,1)} %bitcast.36, bf16[32,512,128]{2,1,0:T(8,128)(2,1)} %subtract_convert_fusion.table, f32[512,4096]{1,0:T(8,128)} %get-tuple-element.22.field, bf16[256,64]{1,0:T(8,128)(2,1)} %bitcast.40, bf16[64,256]{1,0:T(8,128)(2,1)} %get-tuple-element.26.down), custom_call_target="tpu_custom_call" | custom-call | tf_op jit(solution)/shard_map/layer/pallas_call | solution.py:315
  145.9 18.4 %all_to_all.30 = bf16[16,32,512]{2,1,0:T(8,128)(2,1)S(1)} all-to-all(bf16[16,32,512]{2,1,0:T(8,128)(2,1)} %bitcast.39), channel_id=1, replica_groups=mesh['groups'=2,'pen'=16] {'pen'}, dimensions={0} | all-to-all | bytes 1048576 | tf_op jit(solution)/shard_map/all_to_all | solution.py:238
  164.4 0.5 reshape.137
  164.9 0.2 copy.20
  165.1 1.5 reshape.138.data
  166.7 4.4 %mix.3 = bf16[256,1024]{1,0:T(8,128)(2,1)} custom-call(bf16[64,256]{1,0:T(8,128)(2,1)} %constant.60.clone.forward, bf16[256,64]{1,0:T(8,128)(2,1)} %constant.61.clone.inverse, bf16[256,1024]{1,0:T(8,128)(2,1)} %reshape.138.data, bf16[32,1024,128]{2,1,0:T(8,128)(2,1)} %bitcast.28, f32[1,1024]{1,0:T(1,128)} %fusion.2.scaling), custom_call_target="tpu_custom_call" | custom-call | tf_op jit(solution)/shard_map/mix/pallas_call | solution.py:293
  171.0 4.4 %all-to-all-start.4 = ((bf16[16,16,1024]{2,1,0:T(8,128)(2,1)}), bf16[16,16,1024]{2,1,0:T(8,128)(2,1)S(1)}, u32[]{:S(2)}, u32[]{:S(2)}) async-start(bf16[16,16,1024]{2,1,0:T(8,128)(2,1)} %bitcast.35), calls=%async_computation.4 | async-start | bytes 1048576 | tf_op jit(solution)/shard_map/all_to_all | solution.py:238
  175.5 0.7 copy.25
  176.2 13.3 %all-to-all-done.4 = bf16[16,16,1024]{2,1,0:T(8,128)(2,1)S(1)} async-done(((bf16[16,16,1024]{2,1,0:T(8,128)(2,1)}), bf16[16,16,1024]{2,1,0:T(8,128)(2,1)S(1)}, u32[]{:S(2)}, u32[]{:S(2)}) %all-to-all-start.4) | async-done | bytes 524320 | tf_op jit(solution)/shard_map/all_to_all | solution.py:238
  189.5 0.7 reshape.140
  190.1 0.3 copy.21
  190.4 0.6 reshape.141
  191.0 1.0 copy.22
  192.0 14.8 %layer.3.field = bf16[512,4096]{1,0:T(8,128)(2,1)} custom-call(bf16[512,512]{1,0:T(8,128)(2,1)} %bitcast.37, bf16[32,512,128]{2,1,0:T(8,128)(2,1)} %subtract_convert_fusion.table, f32[512,4096]{1,0:T(8,128)} %get-tuple-element.24.field, bf16[256,64]{1,0:T(8,128)(2,1)} %bitcast.41, bf16[64,256]{1,0:T(8,128)(2,1)} %get-tuple-element.25.down), custom_call_target="tpu_custom_call" | custom-call | tf_op jit(solution)/shard_map/layer/pallas_call | solution.py:315
  206.8 4.3 %pick.1 = bf16[16,8,64,128]{3,2,1,0:T(8,128)(2,1)} custom-call(s32[128]{0:T(128)} %reshape.143.targets, bf16[512,4096]{1,0:T(8,128)(2,1)} %layer.3.field), custom_call_target="tpu_custom_call" | custom-call | tf_op jit(solution)/shard_map/pick/pallas_call | solution.py:336
  211.2 52.4 %all_to_all.31 = bf16[16,8,64,128]{3,2,1,0:T(8,128)(2,1)} all-to-all(bf16[16,8,64,128]{3,2,1,0:T(8,128)(2,1)} %pick.1), channel_id=1, replica_groups=mesh['groups'=2,'pen'=16] {'pen'}, dimensions={0} | all-to-all | bytes 4194304 | tf_op jit(solution)/shard_map/all_to_all | solution.py:238
  263.5 6.2 %decode.1 = f32[64,2048]{1,0:T(8,128)} custom-call(s32[64]{0:T(128)} %get-tuple-element.15.slot_of, bf16[128,64,128]{2,1,0:T(8,128)(2,1)} %bitcast.29, bf16[64,128,128]{2,1,0:T(8,128)(2,1)} %kern.3), custom_call_target="tpu_custom_call" | custom-call | tf_op jit(solution)/shard_map/decode/pallas_call | solution.py:344
  (2 shorter events, 0.0 us)
Async XLA Ops:
  6.4 53.4 %all-to-all-start = ((bf16[16,9,64,128]{3,2,1,0:T(8,128)(2,1)}), bf16[16,9,64,128]{3,2,1,0:T(8,128)(2,1)S(1)}, u32[]{:S(2)}, u32[]{:S(2)}) async-start(bf16[16,9,64,128]{3,2,1,0:T(8,128)(2,1)} %get-tuple-element.16), calls=%async_computation | async-start | bytes 4718592 | tf_op jit(solution)/shard_map/all_to_all | solution.py:238
  59.9 1.4 copy-start
  73.6 36.9 %copy-start.1 = (bf16[2,256,64]{1,2,0:T(8,128)(2,1)S(1)}, bf16[2,256,64]{1,2,0:T(8,128)(2,1)}, u32[]{:S(2)}) copy-start(bf16[2,256,64]{1,2,0:T(8,128)(2,1)} %param.18) | copy-start | bytes 196612
  73.6 37.7 %copy-start.2 = (bf16[2,64,256]{2,1,0:T(8,128)(2,1)S(1)}, bf16[2,64,256]{2,1,0:T(8,128)(2,1)}, u32[]{:S(2)}) copy-start(bf16[2,64,256]{2,1,0:T(8,128)(2,1)} %param.19) | copy-start | bytes 196612
  73.6 25.9 %all-to-all-start.1 = ((bf16[16,32,512]{2,1,0:T(8,128)(2,1)}), bf16[16,32,512]{2,1,0:T(8,128)(2,1)S(1)}, u32[]{:S(2)}, u32[]{:S(2)}) async-start(bf16[16,32,512]{2,1,0:T(8,128)(2,1)} %bitcast.38), calls=%async_computation.1 | async-start | bytes 1048576 | tf_op jit(solution)/shard_map/all_to_all | solution.py:238
  106.1 18.4 %all-to-all-start.2 = ((bf16[16,16,1024]{2,1,0:T(8,128)(2,1)}), bf16[16,16,1024]{2,1,0:T(8,128)(2,1)S(1)}, u32[]{:S(2)}, u32[]{:S(2)}) async-start(bf16[16,16,1024]{2,1,0:T(8,128)(2,1)} %bitcast.34), calls=%async_computation.2 | async-start | bytes 1048576 | tf_op jit(solution)/shard_map/all_to_all | solution.py:238
  171.0 18.4 %all-to-all-start.4 = ((bf16[16,16,1024]{2,1,0:T(8,128)(2,1)}), bf16[16,16,1024]{2,1,0:T(8,128)(2,1)S(1)}, u32[]{:S(2)}, u32[]{:S(2)}) async-start(bf16[16,16,1024]{2,1,0:T(8,128)(2,1)} %bitcast.35), calls=%async_computation.4 | async-start | bytes 1048576 | tf_op jit(solution)/shard_map/all_to_all | solution.py:238

commit v3 on v2

--- a/solution.py
+++ b/solution.py
@@ -17,6 +17,8 @@
 MZ = 16
 LAYERS = 2
 NBR = 4
+PARTS = 2
+NOTE_ROWS = 16
 
 F32 = jnp.float32
 BF16 = jnp.bfloat16
@@ -46,14 +48,15 @@
     planes = NX // devices
     waves = np.arange(MX) - MX // 2
     angle = 2 * np.pi * np.mod(np.outer(waves, np.arange(NX)), NX) / NX
-    cos = np.cos(angle).reshape(MX, devices, planes)
-    sin = np.sin(angle).reshape(MX, devices, planes)
-    to_real = np.stack([cos, sin], axis=2)
-    to_imag = np.stack([-sin, cos], axis=2)
-    forward = np.concatenate([to_real, to_imag], axis=0).reshape(2 * MX, 2 * NX)
+    cos = np.cos(angle).reshape(MX, devices, PARTS, planes // PARTS)
+    sin = np.sin(angle).reshape(MX, devices, PARTS, planes // PARTS)
+    to_real = np.stack([cos, sin], axis=3)
+    to_imag = np.stack([-sin, cos], axis=3)
+    forward = np.concatenate([to_real, to_imag], axis=0).transpose(2, 0, 1, 3, 4)
+    forward = forward.reshape(PARTS, 2 * MX, 2 * NX // PARTS)
     high = forward.astype(jnp.bfloat16).astype(np.float64)
-    both = np.concatenate([high, forward - high], axis=0)
-    return jnp.asarray(both, BF16), jnp.asarray(both.T, BF16)
+    both = np.concatenate([high, forward - high], axis=1)
+    return jnp.asarray(both, BF16), jnp.asarray(both.transpose(0, 2, 1), BF16)
 
 
 def encode_kernel(devices, cap, owner, block, feat, kern, send, slot_of, targets, count):
@@ -78,17 +81,18 @@
             count[d] = n + 1
             slot_of[p] = d * cap + n
             targets[d * cap + n] = block[p]
-            send[d, n] = jnp.dot(values, kern[p], preferred_element_type=F32).astype(BF16)
+            rows = pl.ds(pl.multiple_of(n * values.shape[0], values.shape[0]), values.shape[0])
+            send[d, rows, :] = jnp.dot(values, kern[p], preferred_element_type=F32).astype(BF16)
         return carry
 
     lax.fori_loop(0, pairs // NBR, one, 0)
-    lane = lax.broadcasted_iota(jnp.int32, (16, size), 1)
+    lane = lax.broadcasted_iota(jnp.int32, (NOTE_ROWS, size), 1)
 
     def note(d, carry):
-        row = jnp.zeros((16, size), F32)
+        row = jnp.zeros((NOTE_ROWS, size), F32)
         for i in range(cap):
             row = jnp.where(lane == i, targets[d * cap + i].astype(F32), row)
-        send[d, cap, 0:16, :] = row.astype(BF16)
+        send[d, send.shape[1] - NOTE_ROWS :, :] = row.astype(BF16)
         return carry
 
     lax.fori_loop(0, devices, note, 0)
@@ -98,8 +102,9 @@
     return jnp.concatenate([table[k * wide + i] for i in range(wide)], axis=1)
 
 
-def gather_sums_kernel(cap, per_plane, wide, targets, got, table, field, spec, total):
-    channels, size = got.shape[2], got.shape[3]
+def gather_sums_kernel(cap, channels, part, per_plane, wide, targets, got, table, field, spec, total):
+    size = got.shape[2]
+    blocks = field.shape[0] // channels * per_plane
     chunk = wide * size
     tiles = table.shape[0] // wide
 
@@ -111,13 +116,13 @@
 
     def add(d, carry):
         for i in range(cap):
-            t = targets[d * cap + i]
-
-            @pl.when(t >= 0)
+            t = targets[d * cap + i] - part * blocks
+
+            @pl.when((t >= 0) & (t < blocks))
             def _():
                 rows = pl.ds(pl.multiple_of(t // per_plane * channels, channels), channels)
                 cols = pl.ds(pl.multiple_of(t % per_plane * size, size), size)
-                field[rows, cols] += got[d, i].astype(F32)
+                field[rows, cols] += got[d, i * channels : (i + 1) * channels, :].astype(F32)
 
         return carry
 
@@ -133,14 +138,15 @@
     spec[...] = total[...].astype(BF16)
 
 
-def mix_kernel(channels, forward, inverse, data, weight, scaling, out, mixed):
+def mix_kernel(channels, forward, inverse, *refs):
+    datas, (weight, scaling), outs, mixed = refs[:PARTS], refs[PARTS : PARTS + 2], refs[PARTS + 2 : -1], refs[-1]
     rows = 2 * MX
     here, fan = weight.shape[0], weight.shape[1] // (2 * channels)
     width = 2 * channels
     row_wave = lax.broadcasted_iota(jnp.int32, (rows, width), 0) % MX
     half = lax.broadcasted_iota(jnp.int32, (rows, width), 1) // channels
     left = half == 0
-    modes = jnp.dot(forward[...], data[...], preferred_element_type=F32)
+    modes = sum(jnp.dot(forward[i], datas[i][...], preferred_element_type=F32) for i in range(PARTS))
     modes = modes[:rows] + modes[rows:]
     for pair in range(here // 2):
         own = modes[:, pair * width : (pair + 1) * width]
@@ -165,7 +171,8 @@
         both = (both * scaling[:, pair * width : (pair + 1) * width]).astype(BF16)
         mixed[0:rows, pair * width : (pair + 1) * width] = both
         mixed[rows : 2 * rows, pair * width : (pair + 1) * width] = both
-    out[...] = jnp.dot(inverse[...], mixed[...], preferred_element_type=F32).astype(BF16)
+    for i in range(PARTS):
+        outs[i][...] = jnp.dot(inverse[i], mixed[...], preferred_element_type=F32).astype(BF16)
 
 
 def layer_kernel(last, planes, wide, modes, table, field, up, down, out, *rest):
@@ -205,15 +212,23 @@
             spec[...] = total[...].astype(BF16)
 
 
-def pick_kernel(cap, per_plane, targets, field, send):
+def pick_kernel(cap, per_plane, targets, *refs):
+    fields, send = refs[:-1], refs[-1]
     channels, size = send.shape[2], send.shape[3]
+    blocks = fields[0].shape[0] // channels * per_plane
 
     def one(d, carry):
         for i in range(cap):
-            t = jnp.maximum(targets[d * cap + i], 0)
-            rows = pl.ds(pl.multiple_of(t // per_plane * channels, channels), channels)
-            cols = pl.ds(pl.multiple_of(t % per_plane * size, size), size)
-            send[d, i] = field[rows, cols]
+            wanted = jnp.maximum(targets[d * cap + i], 0)
+            for part, field in enumerate(fields):
+                t = wanted - part * blocks
+
+                @pl.when((t >= 0) & (t < blocks))
+                def _():
+                    rows = pl.ds(pl.multiple_of(t // per_plane * channels, channels), channels)
+                    cols = pl.ds(pl.multiple_of(t % per_plane * size, size), size)
+                    send[d, i] = field[rows, cols]
+
         return carry
 
     lax.fori_loop(0, send.shape[0], one, 0)
@@ -232,6 +247,10 @@
         return carry
 
     lax.fori_loop(0, kern.shape[0] // NBR, one, 0)
+
+
+def cost(flops, moved):
+    return pl.CostEstimate(flops=flops, bytes_accessed=moved, transcendentals=0)
 
 
 def swap(values):
@@ -257,7 +276,7 @@
     send, slot_of, targets = pl.pallas_call(
         functools.partial(encode_kernel, devices, cap),
         out_shape=(
-            jax.ShapeDtypeStruct((devices, cap + 1, channels, size), BF16),
+            jax.ShapeDtypeStruct((devices, cap * channels + NOTE_ROWS, size), BF16),
             jax.ShapeDtypeStruct((pairs,), jnp.int32),
             jax.ShapeDtypeStruct((devices * cap,), jnp.int32),
         ),
@@ -267,19 +286,26 @@
         name="encode",
     )(pair_owner[:, 0], pair_block, point_feat, pair_kernel)
     got = swap(send)
-    wanted = got[:, cap, 0, :cap].astype(jnp.int32).reshape(devices * cap)
-
-    field, spec = pl.pallas_call(
-        functools.partial(gather_sums_kernel, cap, per_plane, wide),
-        out_shape=(
-            jax.ShapeDtypeStruct((lines, plane_cells), F32),
-            jax.ShapeDtypeStruct((2 * modes_all, lines), BF16),
-        ),
-        in_specs=[SMEM, VMEM, VMEM],
-        out_specs=(VMEM, VMEM),
-        scratch_shapes=[pltpu.VMEM((2 * modes_all, lines), F32)],
-        name="place",
-    )(wanted, got, table)
+    wanted = got[:, cap * channels, :cap].astype(jnp.int32).reshape(devices * cap)
+
+    lines = lines // PARTS
+    half_planes = planes // PARTS
+    fields, specs = [], []
+    for part in range(PARTS):
+        field, spec = pl.pallas_call(
+            functools.partial(gather_sums_kernel, cap, channels, part, per_plane, wide),
+            out_shape=(
+                jax.ShapeDtypeStruct((lines, plane_cells), F32),
+                jax.ShapeDtypeStruct((2 * modes_all, lines), BF16),
+            ),
+            in_specs=[SMEM, VMEM, VMEM],
+            out_specs=(VMEM, VMEM),
+            scratch_shapes=[pltpu.VMEM((2 * modes_all, lines), F32)],
+            cost_estimate=cost(4 * modes_all * lines * plane_cells, 4 * lines * plane_cells),
+            name="place",
+        )(wanted, got, table)
+        fields.append(field)
+        specs.append(spec)
 
     first_mode = lax.axis_index("pen") * here
     wave_z = (first_mode + jnp.arange(here * channels, dtype=jnp.int32) // channels) % MZ
@@ -288,58 +314,65 @@
     whole = lambda shape: pl.BlockSpec(shape, lambda g: (0,) * len(shape))
     for number in range(LAYERS):
         last = number == LAYERS - 1
-        across = swap(spec.reshape(devices, 2 * here, lines))
-        data = across.reshape(devices, 2, here, planes, channels).transpose(0, 1, 3, 2, 4)
+        datas = []
+        for spec in specs:
+            across = swap(spec.reshape(devices, 2 * here, lines))
+            across = across.reshape(devices, 2, here, half_planes, channels).transpose(0, 1, 3, 2, 4)
+            datas.append(across.reshape(2 * NX // PARTS, here * channels))
+        mixed_shape = (2 * NX // PARTS, here * channels)
         mixed = pl.pallas_call(
             functools.partial(mix_kernel, channels),
-            out_shape=jax.ShapeDtypeStruct((2 * NX, here * channels), BF16),
+            out_shape=(jax.ShapeDtypeStruct(mixed_shape, BF16),) * PARTS,
             grid=(1,),
-            in_specs=[
-                whole((4 * MX, 2 * NX)),
-                whole((2 * NX, 4 * MX)),
-                whole((2 * NX, here * channels)),
+            in_specs=[whole(forward.shape), whole(inverse.shape)]
+            + [whole(mixed_shape)] * PARTS
+            + [
                 pl.BlockSpec((here, MX * channels, 2 * channels), lambda g, n=number: (n, 0, 0)),
                 whole((1, here * channels)),
             ],
-            out_specs=whole((2 * NX, here * channels)),
+            out_specs=(whole(mixed_shape),) * PARTS,
             scratch_shapes=[pltpu.VMEM((4 * MX, here * channels), BF16)],
             name="mix",
-        )(forward, inverse, data.reshape(2 * NX, here * channels), weights, scaling)
-        modes = swap(mixed.reshape(devices, 2 * planes, here * channels))
-        modes = modes.reshape(devices, 2, planes, here, channels).transpose(0, 1, 3, 2, 4)
-        modes = modes.reshape(2 * modes_all, lines).T
+        )(forward, inverse, *datas, weights, scaling)
 
         chunk = wide * size
         spec_shape = (2 * modes_all, lines)
         field_spec = pl.BlockSpec((lines, chunk), lambda k: (0, k))
-        results = pl.pallas_call(
-            functools.partial(layer_kernel, last, planes, wide),
-            out_shape=(jax.ShapeDtypeStruct((lines, plane_cells), BF16 if last else F32),)
-            + (() if last else (jax.ShapeDtypeStruct(spec_shape, BF16),)),
-            grid=(plane_cells // chunk,),
-            in_specs=[
-                pl.BlockSpec((lines, 2 * modes_all), lambda k: (0, 0)),
-                pl.BlockSpec((wide, 2 * modes_all, size), lambda k: (k, 0, 0)),
-                field_spec,
-                pl.BlockSpec((hidden, channels), lambda k: (0, 0)),
-                pl.BlockSpec((channels, hidden), lambda k: (0, 0)),
-            ],
-            out_specs=(field_spec,) + (() if last else (pl.BlockSpec(spec_shape, lambda k: (0, 0)),)),
-            scratch_shapes=[pltpu.VMEM((lines, chunk) if last else spec_shape, F32)],
-            name="layer",
-        )(modes, table, field, mlp_up[number], mlp_down[number])
-        if last:
-            field = results[0]
-        else:
-            field, spec = results
+        specs = []
+        backs = [swap(m.reshape(devices, 2 * half_planes, here * channels)) for m in mixed]
+        for part in range(PARTS):
+            if part:
+                backs[part], fields[part - 1] = lax.optimization_barrier((backs[part], fields[part - 1]))
+            modes = backs[part].reshape(devices, 2, half_planes, here, channels).transpose(0, 1, 3, 2, 4)
+            modes = modes.reshape(2 * modes_all, lines).T
+            results = pl.pallas_call(
+                functools.partial(layer_kernel, last, half_planes, wide),
+                out_shape=(jax.ShapeDtypeStruct((lines, plane_cells), BF16 if last else F32),)
+                + (() if last else (jax.ShapeDtypeStruct(spec_shape, BF16),)),
+                grid=(plane_cells // chunk,),
+                in_specs=[
+                    pl.BlockSpec((lines, 2 * modes_all), lambda k: (0, 0)),
+                    pl.BlockSpec((wide, 2 * modes_all, size), lambda k: (k, 0, 0)),
+                    field_spec,
+                    pl.BlockSpec((hidden, channels), lambda k: (0, 0)),
+                    pl.BlockSpec((channels, hidden), lambda k: (0, 0)),
+                ],
+                out_specs=(field_spec,) + (() if last else (pl.BlockSpec(spec_shape, lambda k: (0, 0)),)),
+                scratch_shapes=[pltpu.VMEM((lines, chunk) if last else spec_shape, F32)],
+                cost_estimate=cost(8 * modes_all * lines * plane_cells, 8 * lines * plane_cells),
+                name="layer",
+            )(modes, table, fields[part], mlp_up[number], mlp_down[number])
+            fields[part] = results[0]
+            if not last:
+                specs.append(results[1])
 
     picked = pl.pallas_call(
         functools.partial(pick_kernel, cap, per_plane),
         out_shape=jax.ShapeDtypeStruct((devices, cap, channels, size), BF16),
-        in_specs=[SMEM, VMEM],
+        in_specs=[SMEM] + [VMEM] * PARTS,
         out_specs=VMEM,
         name="pick",
-    )(wanted, field)
+    )(wanted, *fields)
     fetched = swap(picked).reshape(devices * cap, channels, size)
     return pl.pallas_call(
         decode_kernel,

time: 272 us -> 297 us (1.092)
  waiting for transfers between devices: 77.6 us -> 52 us
  Pallas kernels: 71.6 us -> 94.9 us
  starting transfers between devices: 28.1 us -> 44.1 us
  blocking collectives: 70.8 us -> 80.8 us
  local copies, waits for them, and re-layouts: 13.1 us -> 16.1 us
    all_to_all x4 -> x7, waiting for transfers between devices: 77.6 us -> 52 us  [swap(): lax.all_to_all(values, 'pen', split_axis=0, concat_axis=0, tiled=True)]
    pallas_call x5 -> x8, Pallas kernels: 54.6 us -> 75.5 us  [the longest x4 47.9 us: per_device(): pl.pallas_call(functools.partial(layer_kernel, last, half_planes, wide),...]
    all_to_all x4 -> x7, starting transfers between devices: 28.1 us -> 44.1 us  [swap(): lax.all_to_all(values, 'pen', split_axis=0, concat_axis=0, tiled=True)]
    all_to_all x2 -> x3, blocking collectives: 70.8 us -> 80.8 us  [swap(): lax.all_to_all(values, 'pen', split_axis=0, concat_axis=0, tiled=True)]
    reshape x6 -> x12, local copies, waits for them, and re-layouts: 5.4 us -> 6.54 us  [the longest x4 4.23 us: per_device(): datas.append(across.reshape(2 * NX // PARTS, here * channels))]
  transfers between devices with their start and end apart: 4 -> 7, of which waited for: 4 -> 4; matrix products, arithmetic and copies ran while one was open for 4% -> 6% of each run, Pallas kernels for 0% -> 16%
where the time goes in v3:
time: 297 us; the launch traced here: 295 us
  Pallas kernels  94.9 us (32%)
  blocking collectives  80.8 us (27%)
  waiting for transfers between devices  52 us (18%)
  starting transfers between devices  44.1 us (15%)
  local copies, waits for them, and re-layouts  16.1 us (5%)
  other arithmetic  7.1 us (2%)
    all_to_all x3, blocking collectives, swap(): lax.all_to_all(values, 'pen', split_axis=0, concat_axis=0, tiled=True)  80.8 us
    all_to_all x7, waiting for transfers between devices, swap(): lax.all_to_all(values, 'pen', split_axis=0, concat_axis=0, tiled=True)  52 us
    pallas_call x4, Pallas kernels, per_device(): pl.pallas_call(functools.partial(layer_kernel, last, half_planes, wide),...  47.9 us
    all_to_all x7, starting transfers between devices, swap(): lax.all_to_all(values, 'pen', split_axis=0, concat_axis=0, tiled=True)  44.1 us
    pallas_call x2, Pallas kernels, per_device(): pl.pallas_call(functools.partial(gather_sums_kernel, cap, channels, part,...  18.7 us
    pallas_call x2, Pallas kernels, per_device(): pl.pallas_call(functools.partial(mix_kernel, channels), out_shape=(jax.Sh...  8.85 us
    pallas_call x1, Pallas kernels, per_device(): pl.pallas_call(functools.partial(pick_kernel, cap, per_plane), out_shape=...  6.78 us
    convert_element_type x1, other arithmetic, plane_table(): (cos0[None] * cos_k[:, :, None] - sin0[None] * sin_k[:, :, None]).astype(...  6.45 us
  transfers between devices with their start and end apart: 7, of which 4 were waited for; matrix products, arithmetic and copies ran while one was open for 6% of the time, Pallas kernels for 16%

profile of v3, /device:TPU:1, one launch (start us, length us, event | category | flops | bytes accessed | tf_op | source)
XLA Modules:
  0.0 295.1 jit_solution(5311055545024860577)
XLA Ops:
  0.0 6.4 %encode.1 = (bf16[16,528,128]{2,1,0:T(8,128)(2,1)}, s32[64]{0:T(128)}, s32[128]{0:T(128)}) custom-call(s32[64]{0:T(128)} %bitcast.64, s32[64]{0:T(128)} %block.1, bf16[64,2048]{1,0:T(8,128)(2,1)} %feat.1, bf16[64,128,128]{2,1,0:T(8,128)(2,1)} %kern.3), custom_call_target="tpu_custom_call" | custom-call | tf_op jit(solution)/shard_map/encode/pallas_call | solution.py:276
  6.5 7.3 %all-to-all-start = ((bf16[16,528,128]{2,1,0:T(8,128)(2,1)}), bf16[16,528,128]{2,1,0:T(8,128)(2,1)S(1)}, u32[]{:S(2)}, u32[]{:S(2)}) async-start(bf16[16,528,128]{2,1,0:T(8,128)(2,1)} %get-tuple-element.28), calls=%async_computation | async-start | bytes 4325376 | tf_op jit(solution)/shard_map/all_to_all | solution.py:257
  13.8 6.5 %subtract_convert_fusion.table = bf16[32,512,128]{2,1,0:T(8,128)(2,1)} fusion(f32[32,512]{1,0:T(8,128)S(1)} %copy-done.4, f32[512,128]{1,0:T(8,128)S(1)} %copy-done.2, f32[32,512]{1,0:T(8,128)S(1)} %copy-done.3, f32[512,128]{1,0:T(8,128)S(1)} %copy-done.1), kind=kLoop, calls=%fused_computation | loop fusion | flops 8388608 | bytes 4849664 | tf_op jit(solution)/shard_map/convert_element_type | solution.py:44
  20.3 36.2 %all-to-all-done.got = bf16[16,528,128]{2,1,0:T(8,128)(2,1)S(1)} async-done(((bf16[16,528,128]{2,1,0:T(8,128)(2,1)}), bf16[16,528,128]{2,1,0:T(8,128)(2,1)S(1)}, u32[]{:S(2)}, u32[]{:S(2)}) %all-to-all-start) | async-done | bytes 2162720 | tf_op jit(solution)/shard_map/all_to_all | solution.py:257
  56.5 0.8 reshape.191.targets
  57.3 0.5 copy-done
  57.8 9.4 %place.2 = (f32[256,4096]{1,0:T(8,128)}, bf16[512,256]{1,0:T(8,128)(2,1)}) custom-call(s32[128]{0:T(128)} %reshape.191.targets, bf16[16,528,128]{2,1,0:T(8,128)(2,1)} %copy-done, bf16[32,512,128]{2,1,0:T(8,128)(2,1)} %subtract_convert_fusion.table), custom_call_target="tpu_custom_call" | custom-call | flops 1073741824 | bytes 4194304 | tf_op jit(solution)/shard_map/place/pallas_call | solution.py:295
  67.2 10.9 %all-to-all-start.1 = ((bf16[16,32,256]{2,1,0:T(8,128)(2,1)}), bf16[16,32,256]{2,1,0:T(8,128)(2,1)S(1)}, u32[]{:S(2)}, u32[]{:S(2)}) async-start(bf16[16,32,256]{2,1,0:T(8,128)(2,1)} %bitcast.61), calls=%async_computation.1 | async-start | bytes 524288 | tf_op jit(solution)/shard_map/all_to_all | solution.py:257
  78.1 9.4 %place.3 = (f32[256,4096]{1,0:T(8,128)}, bf16[512,256]{1,0:T(8,128)(2,1)}) custom-call(s32[128]{0:T(128)} %reshape.191.targets, bf16[16,528,128]{2,1,0:T(8,128)(2,1)} %copy-done, bf16[32,512,128]{2,1,0:T(8,128)(2,1)} %subtract_convert_fusion.table), custom_call_target="tpu_custom_call" | custom-call | flops 1073741824 | bytes 4194304 | tf_op jit(solution)/shard_map/place/pallas_call | solution.py:295
  87.6 5.8 %all-to-all-start.2 = ((bf16[16,32,256]{2,1,0:T(8,128)(2,1)}), bf16[16,32,256]{2,1,0:T(8,128)(2,1)S(1)}, u32[]{:S(2)}, u32[]{:S(2)}) async-start(bf16[16,32,256]{2,1,0:T(8,128)(2,1)} %bitcast.57), calls=%async_computation.2 | async-start | bytes 524288 | tf_op jit(solution)/shard_map/all_to_all | solution.py:257
  93.4 0.6 fusion.2.refs_3_
  94.4 1.1 reshape.167.refs_0_
  95.4 7.5 %all-to-all-done.2 = bf16[16,32,256]{2,1,0:T(8,128)(2,1)S(1)} async-done(((bf16[16,32,256]{2,1,0:T(8,128)(2,1)}), bf16[16,32,256]{2,1,0:T(8,128)(2,1)S(1)}, u32[]{:S(2)}, u32[]{:S(2)}) %all-to-all-start.2) | async-done | bytes 262176 | tf_op jit(solution)/shard_map/all_to_all | solution.py:257
  103.3 1.1 reshape.170.refs_1_
  104.3 4.4 %mix.2 = (bf16[128,1024]{1,0:T(8,128)(2,1)}, bf16[128,1024]{1,0:T(8,128)(2,1)}) custom-call(bf16[2,64,128]{2,1,0:T(8,128)(2,1)} %constant.60.clone.forward, bf16[2,128,64]{2,1,0:T(8,128)(2,1)} %constant.61.clone.inverse, bf16[128,1024]{1,0:T(8,128)(2,1)} %reshape.167.refs_0_, bf16[128,1024]{1,0:T(8,128)(2,1)} %reshape.170.refs_1_, ...), custom_call_target="tpu_custom_call" | custom-call | tf_op jit(solution)/shard_map/mix/pallas_call | solution.py:323
  108.8 13.5 %all_to_all.50 = bf16[16,8,1024]{2,1,0:T(8,128)(2,1)S(1)} all-to-all(bf16[16,8,1024]{2,1,0:T(8,128)(2,1)} %bitcast.63), channel_id=1, replica_groups=mesh['groups'=2,'pen'=16] {'pen'}, dimensions={0} | all-to-all | bytes 524288 | tf_op jit(solution)/shard_map/all_to_all | solution.py:257
  122.3 3.9 %all-to-all-start.5 = ((bf16[16,8,1024]{2,1,0:T(8,128)(2,1)}), bf16[16,8,1024]{2,1,0:T(8,128)(2,1)S(1)}, u32[]{:S(2)}, u32[]{:S(2)}) async-start(bf16[16,8,1024]{2,1,0:T(8,128)(2,1)} %bitcast.56), calls=%async_computation.5 | async-start | bytes 524288 | tf_op jit(solution)/shard_map/all_to_all | solution.py:257
  126.2 0.7 copy.30
  126.9 0.6 slice_bitcast_fusion
  127.6 0.3 reshape.173
  127.9 0.3 copy.18
  128.2 0.3 reshape.174
  128.5 0.8 copy.19
  129.4 13.0 %layer.4 = (f32[256,4096]{1,0:T(8,128)}, bf16[512,256]{1,0:T(8,128)(2,1)}) custom-call(bf16[256,512]{1,0:T(8,128)(2,1)} %bitcast.49, bf16[32,512,128]{2,1,0:T(8,128)(2,1)} %subtract_convert_fusion.table, f32[256,4096]{1,0:T(8,128)} %get-tuple-element.36.field, bf16[256,64]{1,0:T(8,128)(2,1)} %bitcast.52, bf16[64,256]{1,0:T(8,128)(2,1)} %get-tuple-element.50.down), custom_call_target="tpu_custom_call" | custom-call | flops 2147483648 | bytes 8388608 | tf_op jit(solution)/shard_map/layer/pallas_call | solution.py:348
  142.4 6.1 %all-to-all-start.4 = ((bf16[16,32,256]{2,1,0:T(8,128)(2,1)}), bf16[16,32,256]{2,1,0:T(8,128)(2,1)S(1)}, u32[]{:S(2)}, u32[]{:S(2)}) async-start(bf16[16,32,256]{2,1,0:T(8,128)(2,1)} %bitcast.58), calls=%async_computation.4 | async-start | bytes 524288 | tf_op jit(solution)/shard_map/all_to_all | solution.py:257
  148.5 0.3 reshape.179
  149.1 0.3 reshape.180
  149.4 0.8 copy.23
  150.3 13.0 %layer.5 = (f32[256,4096]{1,0:T(8,128)}, bf16[512,256]{1,0:T(8,128)(2,1)}) custom-call(bf16[256,512]{1,0:T(8,128)(2,1)} %bitcast.48, bf16[32,512,128]{2,1,0:T(8,128)(2,1)} %subtract_convert_fusion.table, f32[256,4096]{1,0:T(8,128)} %get-tuple-element.41.field, bf16[256,64]{1,0:T(8,128)(2,1)} %bitcast.53, bf16[64,256]{1,0:T(8,128)(2,1)} %get-tuple-element.50.down), custom_call_target="tpu_custom_call" | custom-call | flops 2147483648 | bytes 8388608 | tf_op jit(solution)/shard_map/layer/pallas_call | solution.py:348
  163.3 6.0 %all-to-all-start.6 = ((bf16[16,32,256]{2,1,0:T(8,128)(2,1)}), bf16[16,32,256]{2,1,0:T(8,128)(2,1)S(1)}, u32[]{:S(2)}, u32[]{:S(2)}) async-start(bf16[16,32,256]{2,1,0:T(8,128)(2,1)} %bitcast.60), calls=%async_computation.6 | async-start | bytes 524288 | tf_op jit(solution)/shard_map/all_to_all | solution.py:257
  169.7 1.1 reshape.177.refs_0_
  170.7 8.1 %all-to-all-done.6 = bf16[16,32,256]{2,1,0:T(8,128)(2,1)S(1)} async-done(((bf16[16,32,256]{2,1,0:T(8,128)(2,1)}), bf16[16,32,256]{2,1,0:T(8,128)(2,1)S(1)}, u32[]{:S(2)}, u32[]{:S(2)}) %all-to-all-start.6) | async-done | bytes 262176 | tf_op jit(solution)/shard_map/all_to_all | solution.py:257
  179.2 1.1 reshape.183.refs_1_
  180.2 4.4 %mix.3 = (bf16[128,1024]{1,0:T(8,128)(2,1)}, bf16[128,1024]{1,0:T(8,128)(2,1)}) custom-call(bf16[2,64,128]{2,1,0:T(8,128)(2,1)} %constant.60.clone.forward, bf16[2,128,64]{2,1,0:T(8,128)(2,1)} %constant.61.clone.inverse, bf16[128,1024]{1,0:T(8,128)(2,1)} %reshape.177.refs_0_, bf16[128,1024]{1,0:T(8,128)(2,1)} %reshape.183.refs_1_, ...), custom_call_target="tpu_custom_call" | custom-call | tf_op jit(solution)/shard_map/mix/pallas_call | solution.py:323
  184.6 13.5 %all_to_all.51 = bf16[16,8,1024]{2,1,0:T(8,128)(2,1)S(1)} all-to-all(bf16[16,8,1024]{2,1,0:T(8,128)(2,1)} %bitcast.62), channel_id=1, replica_groups=mesh['groups'=2,'pen'=16] {'pen'}, dimensions={0} | all-to-all | bytes 524288 | tf_op jit(solution)/shard_map/all_to_all | solution.py:257
  198.1 3.9 %all-to-all-start.7 = ((bf16[16,8,1024]{2,1,0:T(8,128)(2,1)}), bf16[16,8,1024]{2,1,0:T(8,128)(2,1)S(1)}, u32[]{:S(2)}, u32[]{:S(2)}) async-start(bf16[16,8,1024]{2,1,0:T(8,128)(2,1)} %bitcast.59), calls=%async_computation.7 | async-start | bytes 524288 | tf_op jit(solution)/shard_map/all_to_all | solution.py:257
  202.0 0.7 copy.31
  202.8 0.3 reshape.186
  203.4 0.3 reshape.187
  203.7 0.8 copy.26
  204.6 11.0 %layer.6.refs_0_ = bf16[256,4096]{1,0:T(8,128)(2,1)} custom-call(bf16[256,512]{1,0:T(8,128)(2,1)} %bitcast.51, bf16[32,512,128]{2,1,0:T(8,128)(2,1)} %subtract_convert_fusion.table, f32[256,4096]{1,0:T(8,128)} %get-tuple-element.45.field, bf16[256,64]{1,0:T(8,128)(2,1)} %bitcast.54, bf16[64,256]{1,0:T(8,128)(2,1)} %get-tuple-element.49.down), custom_call_target="tpu_custom_call" | custom-call | flops 2147483648 | bytes 8388608 | tf_op jit(solution)/shard_map/layer/pallas_call | solution.py:348
  215.5 0.3 reshape.188
  216.1 0.3 reshape.189
  216.5 0.8 copy.29
  217.3 10.9 %layer.7.refs_1_ = bf16[256,4096]{1,0:T(8,128)(2,1)} custom-call(bf16[256,512]{1,0:T(8,128)(2,1)} %bitcast.50, bf16[32,512,128]{2,1,0:T(8,128)(2,1)} %subtract_convert_fusion.table, f32[256,4096]{1,0:T(8,128)} %get-tuple-element.48.field, bf16[256,64]{1,0:T(8,128)(2,1)} %bitcast.55, bf16[64,256]{1,0:T(8,128)(2,1)} %get-tuple-element.49.down), custom_call_target="tpu_custom_call" | custom-call | flops 2147483648 | bytes 8388608 | tf_op jit(solution)/shard_map/layer/pallas_call | solution.py:348
  228.3 6.8 %pick.1 = bf16[16,8,64,128]{3,2,1,0:T(8,128)(2,1)} custom-call(s32[128]{0:T(128)} %reshape.191.targets, bf16[256,4096]{1,0:T(8,128)(2,1)} %layer.6.refs_0_, bf16[256,4096]{1,0:T(8,128)(2,1)} %layer.7.refs_1_), custom_call_target="tpu_custom_call" | custom-call | tf_op jit(solution)/shard_map/pick/pallas_call | solution.py:369
  235.1 53.9 %all_to_all.52 = bf16[16,8,64,128]{3,2,1,0:T(8,128)(2,1)} all-to-all(bf16[16,8,64,128]{3,2,1,0:T(8,128)(2,1)} %pick.1), channel_id=1, replica_groups=mesh['groups'=2,'pen'=16] {'pen'}, dimensions={0} | all-to-all | bytes 4194304 | tf_op jit(solution)/shard_map/all_to_all | solution.py:257
  288.9 6.2 %decode.1 = f32[64,2048]{1,0:T(8,128)} custom-call(s32[64]{0:T(128)} %get-tuple-element.27.slot_of, bf16[128,64,128]{2,1,0:T(8,128)(2,1)} %bitcast.39, bf16[64,128,128]{2,1,0:T(8,128)(2,1)} %kern.3), custom_call_target="tpu_custom_call" | custom-call | tf_op jit(solution)/shard_map/decode/pallas_call | solution.py:377
  (30 shorter events, 2.3 us)
Async XLA Ops:
  0.0 13.8 %copy-start.1 = (f32[512,128]{1,0:T(8,128)S(1)}, f32[512,128]{1,0:T(8,128)}, u32[]{:S(2)}) copy-start(f32[512,128]{1,0:T(8,128)} %constant.56.clone) | copy-start | bytes 786436
  0.0 13.8 %copy-start.2 = (f32[512,128]{1,0:T(8,128)S(1)}, f32[512,128]{1,0:T(8,128)}, u32[]{:S(2)}) copy-start(f32[512,128]{1,0:T(8,128)} %constant.57.clone) | copy-start | bytes 786436
  0.0 13.8 %copy-start.3 = (f32[32,512]{1,0:T(8,128)S(1)}, f32[32,512]{1,0:T(8,128)}, u32[]{:S(2)}) copy-start(f32[32,512]{1,0:T(8,128)} %constant.58.clone) | copy-start | bytes 196612
  0.0 13.8 %copy-start.4 = (f32[32,512]{1,0:T(8,128)S(1)}, f32[32,512]{1,0:T(8,128)}, u32[]{:S(2)}) copy-start(f32[32,512]{1,0:T(8,128)} %constant.59.clone) | copy-start | bytes 196612
  6.5 50.0 %all-to-all-start = ((bf16[16,528,128]{2,1,0:T(8,128)(2,1)}), bf16[16,528,128]{2,1,0:T(8,128)(2,1)S(1)}, u32[]{:S(2)}, u32[]{:S(2)}) async-start(bf16[16,528,128]{2,1,0:T(8,128)(2,1)} %get-tuple-element.28), calls=%async_computation | async-start | bytes 4325376 | tf_op jit(solution)/shard_map/all_to_all | solution.py:257
  56.5 1.3 copy-start
  67.2 20.4 %all-to-all-start.1 = ((bf16[16,32,256]{2,1,0:T(8,128)(2,1)}), bf16[16,32,256]{2,1,0:T(8,128)(2,1)S(1)}, u32[]{:S(2)}, u32[]{:S(2)}) async-start(bf16[16,32,256]{2,1,0:T(8,128)(2,1)} %bitcast.61), calls=%async_computation.1 | async-start | bytes 524288 | tf_op jit(solution)/shard_map/all_to_all | solution.py:257
  87.6 15.3 %all-to-all-start.2 = ((bf16[16,32,256]{2,1,0:T(8,128)(2,1)}), bf16[16,32,256]{2,1,0:T(8,128)(2,1)S(1)}, u32[]{:S(2)}, u32[]{:S(2)}) async-start(bf16[16,32,256]{2,1,0:T(8,128)(2,1)} %bitcast.57), calls=%async_computation.2 | async-start | bytes 524288 | tf_op jit(solution)/shard_map/all_to_all | solution.py:257
  104.3 21.9 %copy-start.5 = (bf16[2,256,64]{1,2,0:T(8,128)(2,1)S(1)}, bf16[2,256,64]{1,2,0:T(8,128)(2,1)}, u32[]{:S(2)}) copy-start(bf16[2,256,64]{1,2,0:T(8,128)(2,1)} %param.18) | copy-start | bytes 196612
  104.3 22.6 %copy-start.6 = (bf16[2,64,256]{2,1,0:T(8,128)(2,1)S(1)}, bf16[2,64,256]{2,1,0:T(8,128)(2,1)}, u32[]{:S(2)}) copy-start(bf16[2,64,256]{2,1,0:T(8,128)(2,1)} %param.19) | copy-start | bytes 196612
  122.3 20.1 %all-to-all-start.5 = ((bf16[16,8,1024]{2,1,0:T(8,128)(2,1)}), bf16[16,8,1024]{2,1,0:T(8,128)(2,1)S(1)}, u32[]{:S(2)}, u32[]{:S(2)}) async-start(bf16[16,8,1024]{2,1,0:T(8,128)(2,1)} %bitcast.56), calls=%async_computation.5 | async-start | bytes 524288 | tf_op jit(solution)/shard_map/all_to_all | solution.py:257
  142.4 20.9 %all-to-all-start.4 = ((bf16[16,32,256]{2,1,0:T(8,128)(2,1)}), bf16[16,32,256]{2,1,0:T(8,128)(2,1)S(1)}, u32[]{:S(2)}, u32[]{:S(2)}) async-start(bf16[16,32,256]{2,1,0:T(8,128)(2,1)} %bitcast.58), calls=%async_computation.4 | async-start | bytes 524288 | tf_op jit(solution)/shard_map/all_to_all | solution.py:257
  163.3 15.5 %all-to-all-start.6 = ((bf16[16,32,256]{2,1,0:T(8,128)(2,1)}), bf16[16,32,256]{2,1,0:T(8,128)(2,1)S(1)}, u32[]{:S(2)}, u32[]{:S(2)}) async-start(bf16[16,32,256]{2,1,0:T(8,128)(2,1)} %bitcast.60), calls=%async_computation.6 | async-start | bytes 524288 | tf_op jit(solution)/shard_map/all_to_all | solution.py:257
  198.1 17.4 %all-to-all-start.7 = ((bf16[16,8,1024]{2,1,0:T(8,128)(2,1)}), bf16[16,8,1024]{2,1,0:T(8,128)(2,1)S(1)}, u32[]{:S(2)}, u32[]{:S(2)}) async-start(bf16[16,8,1024]{2,1,0:T(8,128)(2,1)} %bitcast.59), calls=%async_computation.7 | async-start | bytes 524288 | tf_op jit(solution)/shard_map/all_to_all | solution.py:257

commit v4 on v2

--- a/solution.py
+++ b/solution.py
@@ -17,6 +17,7 @@
 MZ = 16
 LAYERS = 2
 NBR = 4
+NOTE_ROWS = 16
 
 F32 = jnp.float32
 BF16 = jnp.bfloat16
@@ -78,17 +79,18 @@
             count[d] = n + 1
             slot_of[p] = d * cap + n
             targets[d * cap + n] = block[p]
-            send[d, n] = jnp.dot(values, kern[p], preferred_element_type=F32).astype(BF16)
+            rows = pl.ds(pl.multiple_of(n * values.shape[0], values.shape[0]), values.shape[0])
+            send[d, rows, :] = jnp.dot(values, kern[p], preferred_element_type=F32).astype(BF16)
         return carry
 
     lax.fori_loop(0, pairs // NBR, one, 0)
-    lane = lax.broadcasted_iota(jnp.int32, (16, size), 1)
+    lane = lax.broadcasted_iota(jnp.int32, (NOTE_ROWS, size), 1)
 
     def note(d, carry):
-        row = jnp.zeros((16, size), F32)
+        row = jnp.zeros((NOTE_ROWS, size), F32)
         for i in range(cap):
             row = jnp.where(lane == i, targets[d * cap + i].astype(F32), row)
-        send[d, cap, 0:16, :] = row.astype(BF16)
+        send[d, send.shape[1] - NOTE_ROWS :, :] = row.astype(BF16)
         return carry
 
     lax.fori_loop(0, devices, note, 0)
@@ -98,8 +100,8 @@
     return jnp.concatenate([table[k * wide + i] for i in range(wide)], axis=1)
 
 
-def gather_sums_kernel(cap, per_plane, wide, targets, got, table, field, spec, total):
-    channels, size = got.shape[2], got.shape[3]
+def gather_sums_kernel(cap, channels, per_plane, wide, targets, got, table, field, spec, total):
+    size = got.shape[2]
     chunk = wide * size
     tiles = table.shape[0] // wide
 
@@ -117,7 +119,7 @@
             def _():
                 rows = pl.ds(pl.multiple_of(t // per_plane * channels, channels), channels)
                 cols = pl.ds(pl.multiple_of(t % per_plane * size, size), size)
-                field[rows, cols] += got[d, i].astype(F32)
+                field[rows, cols] += got[d, i * channels : (i + 1) * channels, :].astype(F32)
 
         return carry
 
@@ -257,7 +259,7 @@
     send, slot_of, targets = pl.pallas_call(
         functools.partial(encode_kernel, devices, cap),
         out_shape=(
-            jax.ShapeDtypeStruct((devices, cap + 1, channels, size), BF16),
+            jax.ShapeDtypeStruct((devices, cap * channels + NOTE_ROWS, size), BF16),
             jax.ShapeDtypeStruct((pairs,), jnp.int32),
             jax.ShapeDtypeStruct((devices * cap,), jnp.int32),
         ),
@@ -267,10 +269,10 @@
         name="encode",
     )(pair_owner[:, 0], pair_block, point_feat, pair_kernel)
     got = swap(send)
-    wanted = got[:, cap, 0, :cap].astype(jnp.int32).reshape(devices * cap)
+    wanted = got[:, cap * channels, :cap].astype(jnp.int32).reshape(devices * cap)
 
     field, spec = pl.pallas_call(
-        functools.partial(gather_sums_kernel, cap, per_plane, wide),
+        functools.partial(gather_sums_kernel, cap, channels, per_plane, wide),
         out_shape=(
             jax.ShapeDtypeStruct((lines, plane_cells), F32),
             jax.ShapeDtypeStruct((2 * modes_all, lines), BF16),

time: 272 us -> 267 us (0.982)
  waiting for transfers between devices: 77.6 us -> 74.2 us
    all_to_all x4, waiting for transfers between devices: 77.6 us -> 74.2 us  [swap(): lax.all_to_all(values, 'pen', split_axis=0, concat_axis=0, tiled=True)]
where the time goes in v4:
time: 267 us; the launch traced here: 266 us
  waiting for transfers between devices  74.2 us (28%)
  Pallas kernels  71.7 us (27%)
  blocking collectives  70.8 us (27%)
  starting transfers between devices  27.6 us (10%)
  local copies, waits for them, and re-layouts  13.1 us (5%)
  other arithmetic  8.39 us (3%)
    all_to_all x4, waiting for transfers between devices, swap(): lax.all_to_all(values, 'pen', split_axis=0, concat_axis=0, tiled=True)  74.2 us
    all_to_all x2, blocking collectives, swap(): lax.all_to_all(values, 'pen', split_axis=0, concat_axis=0, tiled=True)  70.8 us
    pallas_call x2, Pallas kernels, per_device(): pl.pallas_call(functools.partial(layer_kernel, last, planes, wide), out_s...  33.6 us
    all_to_all x4, starting transfers between devices, swap(): lax.all_to_all(values, 'pen', split_axis=0, concat_axis=0, tiled=True)  27.6 us
    pallas_call x1, Pallas kernels, per_device(): pl.pallas_call(functools.partial(gather_sums_kernel, cap, channels, per_p...  12.4 us
    pallas_call x2, Pallas kernels, per_device(): pl.pallas_call(functools.partial(mix_kernel, channels), out_shape=jax.Sha...  8.74 us
    convert_element_type x1, other arithmetic, plane_table(): (cos0[None] * cos_k[:, :, None] - sin0[None] * sin_k[:, :, None]).astype(...  7.74 us
    pallas_call x1, Pallas kernels, per_device(): pl.pallas_call(functools.partial(encode_kernel, devices, cap), out_shape=...  6.35 us
  transfers between devices with their start and end apart: 4, of which 4 were waited for; matrix products, arithmetic and copies ran while one was open for 4% of the time, Pallas kernels for 0%

profile of v4, /device:TPU:1, one launch (start us, length us, event | category | flops | bytes accessed | tf_op | source)
XLA Modules:
  0.0 265.8 jit_solution(10909692110295504091)
XLA Ops:
  0.0 6.3 %encode.1 = (bf16[16,528,128]{2,1,0:T(8,128)(2,1)}, s32[64]{0:T(128)}, s32[128]{0:T(128)}) custom-call(s32[64]{0:T(128)} %bitcast.42, s32[64]{0:T(128)} %block.1, bf16[64,2048]{1,0:T(8,128)(2,1)} %feat.1, bf16[64,128,128]{2,1,0:T(8,128)(2,1)} %kern.3), custom_call_target="tpu_custom_call" | custom-call | tf_op jit(solution)/shard_map/encode/pallas_call | solution.py:259
  6.4 7.3 %all-to-all-start = ((bf16[16,528,128]{2,1,0:T(8,128)(2,1)}), bf16[16,528,128]{2,1,0:T(8,128)(2,1)S(1)}, u32[]{:S(2)}, u32[]{:S(2)}) async-start(bf16[16,528,128]{2,1,0:T(8,128)(2,1)} %get-tuple-element.16), calls=%async_computation | async-start | bytes 4325376 | tf_op jit(solution)/shard_map/all_to_all | solution.py:240
  13.7 7.7 %subtract_convert_fusion.table = bf16[32,512,128]{2,1,0:T(8,128)(2,1)} fusion(f32[32,512]{1,0:T(8,128)} %constant.59.clone, f32[512,128]{1,0:T(8,128)} %constant.57.clone, f32[32,512]{1,0:T(8,128)} %constant.58.clone, f32[512,128]{1,0:T(8,128)} %constant.56.clone), kind=kLoop, calls=%fused_computation | loop fusion | flops 8388608 | bytes 4849664 | tf_op jit(solution)/shard_map/convert_element_type | solution.py:43
  21.4 34.9 %all-to-all-done.got = bf16[16,528,128]{2,1,0:T(8,128)(2,1)S(1)} async-done(((bf16[16,528,128]{2,1,0:T(8,128)(2,1)}), bf16[16,528,128]{2,1,0:T(8,128)(2,1)S(1)}, u32[]{:S(2)}, u32[]{:S(2)}) %all-to-all-start) | async-done | bytes 2162720 | tf_op jit(solution)/shard_map/all_to_all | solution.py:240
  56.4 0.0 copy-start
  56.4 0.8 reshape.143.targets
  57.2 0.5 copy-done
  57.7 12.4 %place.1 = (f32[512,4096]{1,0:T(8,128)}, bf16[512,512]{1,0:T(8,128)(2,1)}) custom-call(s32[128]{0:T(128)} %reshape.143.targets, bf16[16,528,128]{2,1,0:T(8,128)(2,1)} %copy-done, bf16[32,512,128]{2,1,0:T(8,128)(2,1)} %subtract_convert_fusion.table), custom_call_target="tpu_custom_call" | custom-call | tf_op jit(solution)/shard_map/place/pallas_call | solution.py:274
  70.2 0.0 copy-start.1
  70.2 0.0 copy-start.2
  70.2 11.4 %all-to-all-start.1 = ((bf16[16,32,512]{2,1,0:T(8,128)(2,1)}), bf16[16,32,512]{2,1,0:T(8,128)(2,1)S(1)}, u32[]{:S(2)}, u32[]{:S(2)}) async-start(bf16[16,32,512]{2,1,0:T(8,128)(2,1)} %bitcast.38), calls=%async_computation.1 | async-start | bytes 1048576 | tf_op jit(solution)/shard_map/all_to_all | solution.py:240
  81.5 0.6 fusion.2.scaling
  82.2 13.4 %all-to-all-done.1 = bf16[16,32,512]{2,1,0:T(8,128)(2,1)S(1)} async-done(((bf16[16,32,512]{2,1,0:T(8,128)(2,1)}), bf16[16,32,512]{2,1,0:T(8,128)(2,1)S(1)}, u32[]{:S(2)}, u32[]{:S(2)}) %all-to-all-start.1) | async-done | bytes 524320 | tf_op jit(solution)/shard_map/all_to_all | solution.py:240
  95.5 0.5 reshape.130
  96.1 0.2 copy.16
  96.3 1.5 reshape.131.data
  97.8 4.3 %mix.2 = bf16[256,1024]{1,0:T(8,128)(2,1)} custom-call(bf16[64,256]{1,0:T(8,128)(2,1)} %constant.60.clone.forward, bf16[256,64]{1,0:T(8,128)(2,1)} %constant.61.clone.inverse, bf16[256,1024]{1,0:T(8,128)(2,1)} %reshape.131.data, bf16[32,1024,128]{2,1,0:T(8,128)(2,1)} %bitcast.27, f32[1,1024]{1,0:T(1,128)} %fusion.2.scaling), custom_call_target="tpu_custom_call" | custom-call | tf_op jit(solution)/shard_map/mix/pallas_call | solution.py:295
  102.2 4.4 %all-to-all-start.2 = ((bf16[16,16,1024]{2,1,0:T(8,128)(2,1)}), bf16[16,16,1024]{2,1,0:T(8,128)(2,1)S(1)}, u32[]{:S(2)}, u32[]{:S(2)}) async-start(bf16[16,16,1024]{2,1,0:T(8,128)(2,1)} %bitcast.34), calls=%async_computation.2 | async-start | bytes 1048576 | tf_op jit(solution)/shard_map/all_to_all | solution.py:240
  106.6 0.0 copy-done.1
  106.6 0.7 copy.24
  107.4 0.0 copy-done.2
  107.4 0.6 slice_bitcast_fusion
  108.0 12.6 %all-to-all-done.2 = bf16[16,16,1024]{2,1,0:T(8,128)(2,1)S(1)} async-done(((bf16[16,16,1024]{2,1,0:T(8,128)(2,1)}), bf16[16,16,1024]{2,1,0:T(8,128)(2,1)S(1)}, u32[]{:S(2)}, u32[]{:S(2)}) %all-to-all-start.2) | async-done | bytes 524320 | tf_op jit(solution)/shard_map/all_to_all | solution.py:240
  120.6 0.7 reshape.134
  121.3 0.3 copy.17
  121.6 0.6 reshape.135
  122.2 1.0 copy.18
  123.2 18.8 %layer.2 = (f32[512,4096]{1,0:T(8,128)}, bf16[512,512]{1,0:T(8,128)(2,1)}) custom-call(bf16[512,512]{1,0:T(8,128)(2,1)} %bitcast.36, bf16[32,512,128]{2,1,0:T(8,128)(2,1)} %subtract_convert_fusion.table, f32[512,4096]{1,0:T(8,128)} %get-tuple-element.22.field, bf16[256,64]{1,0:T(8,128)(2,1)} %bitcast.40, bf16[64,256]{1,0:T(8,128)(2,1)} %get-tuple-element.26.down), custom_call_target="tpu_custom_call" | custom-call | tf_op jit(solution)/shard_map/layer/pallas_call | solution.py:317
  142.0 18.4 %all_to_all.30 = bf16[16,32,512]{2,1,0:T(8,128)(2,1)S(1)} all-to-all(bf16[16,32,512]{2,1,0:T(8,128)(2,1)} %bitcast.39), channel_id=1, replica_groups=mesh['groups'=2,'pen'=16] {'pen'}, dimensions={0} | all-to-all | bytes 1048576 | tf_op jit(solution)/shard_map/all_to_all | solution.py:240
  160.5 0.5 reshape.137
  161.0 0.2 copy.20
  161.2 1.5 reshape.138.data
  162.8 4.4 %mix.3 = bf16[256,1024]{1,0:T(8,128)(2,1)} custom-call(bf16[64,256]{1,0:T(8,128)(2,1)} %constant.60.clone.forward, bf16[256,64]{1,0:T(8,128)(2,1)} %constant.61.clone.inverse, bf16[256,1024]{1,0:T(8,128)(2,1)} %reshape.138.data, bf16[32,1024,128]{2,1,0:T(8,128)(2,1)} %bitcast.28, f32[1,1024]{1,0:T(1,128)} %fusion.2.scaling), custom_call_target="tpu_custom_call" | custom-call | tf_op jit(solution)/shard_map/mix/pallas_call | solution.py:295
  167.1 4.4 %all-to-all-start.4 = ((bf16[16,16,1024]{2,1,0:T(8,128)(2,1)}), bf16[16,16,1024]{2,1,0:T(8,128)(2,1)S(1)}, u32[]{:S(2)}, u32[]{:S(2)}) async-start(bf16[16,16,1024]{2,1,0:T(8,128)(2,1)} %bitcast.35), calls=%async_computation.4 | async-start | bytes 1048576 | tf_op jit(solution)/shard_map/all_to_all | solution.py:240
  171.6 0.7 copy.25
  172.3 13.3 %all-to-all-done.4 = bf16[16,16,1024]{2,1,0:T(8,128)(2,1)S(1)} async-done(((bf16[16,16,1024]{2,1,0:T(8,128)(2,1)}), bf16[16,16,1024]{2,1,0:T(8,128)(2,1)S(1)}, u32[]{:S(2)}, u32[]{:S(2)}) %all-to-all-start.4) | async-done | bytes 524320 | tf_op jit(solution)/shard_map/all_to_all | solution.py:240
  185.6 0.7 reshape.140
  186.2 0.3 copy.21
  186.5 0.6 reshape.141
  187.1 1.0 copy.22
  188.1 14.8 %layer.3.field = bf16[512,4096]{1,0:T(8,128)(2,1)} custom-call(bf16[512,512]{1,0:T(8,128)(2,1)} %bitcast.37, bf16[32,512,128]{2,1,0:T(8,128)(2,1)} %subtract_convert_fusion.table, f32[512,4096]{1,0:T(8,128)} %get-tuple-element.24.field, bf16[256,64]{1,0:T(8,128)(2,1)} %bitcast.41, bf16[64,256]{1,0:T(8,128)(2,1)} %get-tuple-element.25.down), custom_call_target="tpu_custom_call" | custom-call | tf_op jit(solution)/shard_map/layer/pallas_call | solution.py:317
  202.9 4.3 %pick.1 = bf16[16,8,64,128]{3,2,1,0:T(8,128)(2,1)} custom-call(s32[128]{0:T(128)} %reshape.143.targets, bf16[512,4096]{1,0:T(8,128)(2,1)} %layer.3.field), custom_call_target="tpu_custom_call" | custom-call | tf_op jit(solution)/shard_map/pick/pallas_call | solution.py:338
  207.3 52.4 %all_to_all.31 = bf16[16,8,64,128]{3,2,1,0:T(8,128)(2,1)} all-to-all(bf16[16,8,64,128]{3,2,1,0:T(8,128)(2,1)} %pick.1), channel_id=1, replica_groups=mesh['groups'=2,'pen'=16] {'pen'}, dimensions={0} | all-to-all | bytes 4194304 | tf_op jit(solution)/shard_map/all_to_all | solution.py:240
  259.6 6.2 %decode.1 = f32[64,2048]{1,0:T(8,128)} custom-call(s32[64]{0:T(128)} %get-tuple-element.15.slot_of, bf16[128,64,128]{2,1,0:T(8,128)(2,1)} %bitcast.29, bf16[64,128,128]{2,1,0:T(8,128)(2,1)} %kern.3), custom_call_target="tpu_custom_call" | custom-call | tf_op jit(solution)/shard_map/decode/pallas_call | solution.py:346
  (2 shorter events, 0.0 us)
Async XLA Ops:
  6.4 50.0 %all-to-all-start = ((bf16[16,528,128]{2,1,0:T(8,128)(2,1)}), bf16[16,528,128]{2,1,0:T(8,128)(2,1)S(1)}, u32[]{:S(2)}, u32[]{:S(2)}) async-start(bf16[16,528,128]{2,1,0:T(8,128)(2,1)} %get-tuple-element.16), calls=%async_computation | async-start | bytes 4325376 | tf_op jit(solution)/shard_map/all_to_all | solution.py:240
  56.4 1.4 copy-start
  70.2 36.5 %copy-start.1 = (bf16[2,256,64]{1,2,0:T(8,128)(2,1)S(1)}, bf16[2,256,64]{1,2,0:T(8,128)(2,1)}, u32[]{:S(2)}) copy-start(bf16[2,256,64]{1,2,0:T(8,128)(2,1)} %param.18) | copy-start | bytes 196612
  70.2 37.2 %copy-start.2 = (bf16[2,64,256]{2,1,0:T(8,128)(2,1)S(1)}, bf16[2,64,256]{2,1,0:T(8,128)(2,1)}, u32[]{:S(2)}) copy-start(bf16[2,64,256]{2,1,0:T(8,128)(2,1)} %param.19) | copy-start | bytes 196612
  70.2 25.4 %all-to-all-start.1 = ((bf16[16,32,512]{2,1,0:T(8,128)(2,1)}), bf16[16,32,512]{2,1,0:T(8,128)(2,1)S(1)}, u32[]{:S(2)}, u32[]{:S(2)}) async-start(bf16[16,32,512]{2,1,0:T(8,128)(2,1)} %bitcast.38), calls=%async_computation.1 | async-start | bytes 1048576 | tf_op jit(solution)/shard_map/all_to_all | solution.py:240
  102.2 18.4 %all-to-all-start.2 = ((bf16[16,16,1024]{2,1,0:T(8,128)(2,1)}), bf16[16,16,1024]{2,1,0:T(8,128)(2,1)S(1)}, u32[]{:S(2)}, u32[]{:S(2)}) async-start(bf16[16,16,1024]{2,1,0:T(8,128)(2,1)} %bitcast.34), calls=%async_computation.2 | async-start | bytes 1048576 | tf_op jit(solution)/shard_map/all_to_all | solution.py:240
  167.1 18.4 %all-to-all-start.4 = ((bf16[16,16,1024]{2,1,0:T(8,128)(2,1)}), bf16[16,16,1024]{2,1,0:T(8,128)(2,1)S(1)}, u32[]{:S(2)}, u32[]{:S(2)}) async-start(bf16[16,16,1024]{2,1,0:T(8,128)(2,1)} %bitcast.35), calls=%async_computation.4 | async-start | bytes 1048576 | tf_op jit(solution)/shard_map/all_to_all | solution.py:240
